TPU v7x, 32 devices: a whole 2x2x4 slice. The times are simulated.
32 devices in a mesh: box: 4 (over y, core), dir: 8 (over z, x).
Axes of the slice: x: 2, y: 2, z: 4, core: 2. Of those that a mesh axis runs over, the one named last changes fastest.
Arguments:
- child_rad: float32 [64, 2, 128, 256], P('box', None, 'dir'), may hold values from -6 to 6
- parent_incoming: float32 [16, 2, 256, 512], P('box', None, 'dir'), may hold values from -6 to 6
- theta_interp: float32 [256, 128], replicated, may hold values from -0.5 to 0.5
- phi_interp: float32 [256, 512], replicated, may hold values from -0.375 to 0.375
- child_ops: float32 [40, 2, 128, 256], P(None, None, 'dir'), may hold values from -2 to 2
- parent_ops: float32 [40, 2, 256, 512], P(None, None, 'dir'), may hold values from -2 to 2
- child_parent: int32 [64], P('box'), may hold values from 0 to 15, as said below
- child_octant: int32 [64], P('box'), may hold values from 0 to 7, as said below
- far_child_src: int32 [64, 16], P('box'), may hold values from 0 to 63, as said below
- far_child_op: int32 [64, 16], P('box'), may hold values from 0 to 39
- far_child_len: int32 [64], P('box'), may hold values from 1 to 16
- far_parent_src: int32 [16, 8], P('box'), may hold values from 0 to 15, as said below
- far_parent_op: int32 [16, 8], P('box'), may hold values from 0 to 39
- far_parent_len: int32 [16], P('box'), may hold values from 1 to 8
Outputs:
- child_local: float32 [64, 2, 128, 256], P('box', None, 'dir')
- parent_local: float32 [16, 2, 256, 512], P('box', None, 'dir')
- parent_rad: float32 [16, 2, 256, 512], P('box', None, 'dir')
Inputs may be any that keep to these rules, and one draw needn't show every extreme that they name: child_parent never falls; the children of parents 4 q to 4 q + 3 are exactly children 16 q to 16 q + 15, every parent has 2 to 6 children. `child_octant`: children of one parent have distinct octants. far_child_src[c, k] differs from c, and far_child_src[c, k] // 16 differs from c // 16 by at most 1. far_parent_src[p, k] differs from p, and far_parent_src[p, k] // 4 differs from p // 4 by at most 1.
All inputs are finite; a program needn't handle non-finite values.
Results may differ from a plain program's by a relative error of at most 0.0003.
Values sent between devices are 32-bit elements; how exact they have to be, the bound alone decides.
A program may use at most 64 MiB of HBM per device.

v0:
```python
import math

import jax
import jax.numpy as jnp
from jax import lax
from jax.sharding import PartitionSpec as P

phase_scale = 6.0
highest = lax.Precision.HIGHEST


def extended_2(array, sides, width):
    for axis, dim in sides:
        size, length = (lax.axis_size(axis), array.shape[dim])
        up = [(i, (i + 1) % size) for i in range(size - 1)]
        down = [(j, i) for i, j in up]
        last = lax.slice_in_dim(array, length - width, length, axis=dim)
        initial = lax.slice_in_dim(array, 0, width, axis=dim)
        before = lax.ppermute(last, axis, up)
        after = lax.ppermute(initial, axis, down)
        array = jnp.concatenate([before, array, after], axis=dim)
    return array


def octant_signs(octant):
    first = 1.0 - 2.0 * (octant % 2).astype(jnp.float32)
    second = 1.0 - 2.0 * (octant // 2 % 2).astype(jnp.float32)
    third = 1.0 - 2.0 * (octant // 4 % 2).astype(jnp.float32)
    return (first, second, third)


def phase_block(octant, row_start, row_count, total_rows, col_start, col_count, total_cols):
    angle_rows = (row_start + jnp.arange(row_count, dtype=jnp.int32)).astype(jnp.float32)
    theta = math.pi * (angle_rows + 0.5) / total_rows
    angle_cols = (col_start + jnp.arange(col_count, dtype=jnp.int32)).astype(jnp.float32)
    azimuth = 2.0 * math.pi * angle_cols / total_cols
    sin_theta = jnp.sin(theta)[:, None]
    along_x = sin_theta * jnp.cos(azimuth)[None, :]
    along_y = sin_theta * jnp.sin(azimuth)[None, :]
    along_z = jnp.cos(theta)[:, None] + 0.0 * azimuth[None, :]
    first, second, third = octant_signs(octant)
    argument = phase_scale * (
        first[:, None, None] * along_x
        + second[:, None, None] * along_y
        + third[:, None, None] * along_z
    )
    return (jnp.cos(argument), jnp.sin(argument))


def phase_parts(octant, row_start, row_count, total_rows, col_count):
    return phase_block(octant, row_start, row_count, total_rows, 0, col_count, col_count)


def translate(extended, operators, source, which_op, length, offset):
    position = source - offset
    picked = extended[position]
    chosen = operators[which_op]
    live = (jnp.arange(source.shape[1], dtype=jnp.int32)[None, :] < length[:, None]).astype(
        jnp.float32
    )[:, :, None, None]
    real_part = jnp.sum(
        live * (chosen[:, :, 0] * picked[:, :, 0] - chosen[:, :, 1] * picked[:, :, 1]), axis=1
    )
    imag_part = jnp.sum(
        live * (chosen[:, :, 0] * picked[:, :, 1] + chosen[:, :, 1] * picked[:, :, 0]), axis=1
    )
    return jnp.stack([real_part, imag_part], axis=1)


def per_device(
    child_rad,
    parent_incoming,
    theta_interp,
    phi_interp,
    child_ops,
    parent_ops,
    child_parent,
    child_octant,
    far_child_src,
    far_child_op,
    far_child_len,
    far_parent_src,
    far_parent_op,
    far_parent_len,
):
    child_count = child_rad.shape[0]
    parent_count = parent_incoming.shape[0]
    theta_parent = parent_incoming.shape[2]
    phi_parent = parent_incoming.shape[3]
    theta_total = theta_interp.shape[0]
    dir_count = lax.axis_size("dir")
    phi_slice = phi_parent // dir_count
    box_index = lax.axis_index("box")
    dir_index = lax.axis_index("dir")
    parent_slot = child_parent - box_index * parent_count
    member = (parent_slot[None, :] == jnp.arange(parent_count, dtype=jnp.int32)[:, None]).astype(
        jnp.float32
    )
    child_wide = extended_2(child_rad, (("box", 0),), child_count)
    child_offset = (box_index - 1) * child_count
    child_trans = translate(
        child_wide, child_ops, far_child_src, far_child_op, far_child_len, child_offset
    )
    theta_mine = lax.dynamic_slice_in_dim(theta_interp, dir_index * theta_parent, theta_parent, 0)
    theta_done = jnp.einsum(
        "jt,nctf->ncjf",
        theta_mine,
        lax.all_gather(child_rad, "dir", axis=2, tiled=True),
        precision=highest,
    )
    interp = jnp.einsum("ncjf,fg->ncjg", theta_done, phi_interp, precision=highest)
    cosine, sine = phase_parts(
        child_octant, dir_index * theta_parent, theta_parent, theta_total, phi_parent
    )
    shifted = jnp.stack(
        [cosine * interp[:, 0] - sine * interp[:, 1], sine * interp[:, 0] + cosine * interp[:, 1]],
        axis=1,
    )
    parent_rad = jnp.einsum("pn,ncjg->pcjg", member, shifted, precision=highest)
    parent_wide = extended_2(parent_rad, (("box", 0),), parent_count)
    parent_offset = (box_index - 1) * parent_count
    parent_local = parent_incoming + translate(
        parent_wide, parent_ops, far_parent_src, far_parent_op, far_parent_len, parent_offset
    )
    parent_cols = lax.all_to_all(parent_local, "dir", split_axis=3, concat_axis=2, tiled=True)
    own_field = parent_cols[parent_slot]
    cosine, sine = phase_block(
        child_octant, 0, theta_total, theta_total, dir_index * phi_slice, phi_slice, phi_parent
    )
    unshift = jnp.stack(
        [
            cosine * own_field[:, 0] + sine * own_field[:, 1],
            cosine * own_field[:, 1] - sine * own_field[:, 0],
        ],
        axis=1,
    )
    back_cols = jnp.einsum("jt,ncjg->nctg", theta_interp, unshift, precision=highest)
    back_theta = lax.all_to_all(back_cols, "dir", split_axis=2, concat_axis=3, tiled=True)
    anterp = jnp.einsum("nctg,fg->nctf", back_theta, phi_interp, precision=highest)
    child_local = child_trans + anterp
    return (child_local, parent_local, parent_rad)


def solution(mesh):
    in_specs = (
        P("box", None, "dir", None),
        P("box", None, "dir", None),
        P(),
        P(),
        P(None, None, "dir", None),
        P(None, None, "dir", None),
        P("box"),
        P("box"),
        P("box", None),
        P("box", None),
        P("box"),
        P("box", None),
        P("box", None),
        P("box"),
    )
    out_specs = (
        P("box", None, "dir", None),
        P("box", None, "dir", None),
        P("box", None, "dir", None),
    )
    return jax.shard_map(
        per_device, mesh=mesh, in_specs=in_specs, out_specs=out_specs, check_vma=False
    )
```

profile of v0, /device:TPU:1, one launch (start us, length us, event | category | flops | bytes accessed | tf_op | source)
XLA Modules:
  0.0 217.1 jit_solution(12554408087292023195)
XLA Ops:
  10.3 73.6 %all-gather.2.cloned.1.call-done = f32[16,2,128,256]{3,2,1,0:T(8,128)} async-done(((f32[16,2,16,256]{3,2,1,0:T(8,128)}), f32[16,2,128,256]{3,2,1,0:T(8,128)}) %all-gather.2.cloned.1.call-update) | async-done | bytes 4194320 | tf_op jit(solution)/shard_map/all_gather | solution.py:108
  83.8 4.0 %convolution_bitcast_fusion = f32[16,2,32,256]{3,2,1,0:T(8,128)S(1)} fusion(f32[16,2,128,256]{3,2,1,0:T(8,128)} %all-gather.2.cloned.1.call-done, f32[256,128]{1,0:T(8,128)} %param.16, s32[]{:T(128)S(6)} %select_n.57), kind=kOutput, calls=%fused_computation.34 | convolution fusion | flops 402653184 | bytes 5259268 | tf_op jit(solution)/shard_map/jt,nctf->ncjf/dot_general | solution.py:105
  89.6 4.3 %multiply_subtract_fusion.1 = (f32[16,1,32,512]{3,2,1,0:T(8,128)S(1)}, f32[16,1,32,512]{3,2,1,0:T(8,128)S(1)}) fusion(f32[16,2,32,512]{3,2,1,0:T(8,128)S(1)} %fusion.21, f32[32,512]{1,0:T(8,128)S(1)} %broadcast_add_fusion, f32[16]{0:T(128)S(1)} %get-tuple-element.32, f32[32,512]{1,0:T(8,128)S(1)} %get-tuple-element.34, f32[16]{0:T(128)S(1)} %get-tuple-element.31, ...), kind=kLoop, calls=%fused_computation.39 | loop fusion | flops 3145728 | bytes 4391104 | tf_op jit(solution)/shard_map/sub | solution.py:116
  96.2 3.8 %collective-permute-start.3 = (f32[4,2,32,512]{3,0,2,1:T(4,128)S(1)}, f32[4,2,32,512]{3,0,2,1:T(4,128)S(1)}, u32[]{:S(2)}, u32[]{:S(2)}) collective-permute-start(f32[4,2,32,512]{3,0,2,1:T(4,128)S(1)} %fusion.11), channel_id=1, source_target_pairs={{8,0},{16,8},{24,16},{9,1},{17,9},{25,17},{10,2},{18,10},{26,18},{... | collective-permute-start | bytes 1572872 | tf_op jit(solution)/shard_map/ppermute | solution.py:20
  100.0 3.2 %collective-permute-start.2 = (f32[4,2,32,512]{3,0,2,1:T(4,128)S(1)}, f32[4,2,32,512]{3,0,2,1:T(4,128)S(1)}, u32[]{:S(2)}, u32[]{:S(2)}) collective-permute-start(f32[4,2,32,512]{3,0,2,1:T(4,128)S(1)} %fusion.11), channel_id=1, source_target_pairs={{0,8},{8,16},{16,24},{1,9},{9,17},{17,25},{2,10},{10,18},{18,26},{... | collective-permute-start | bytes 1572872 | tf_op jit(solution)/shard_map/ppermute | solution.py:19
  103.4 5.3 %gather_fusion.2 = f32[32,2,32,512]{3,2,1,0:T(8,128)} fusion(f32[40,2,32,512]{3,2,1,0:T(8,128)} %param.19, s32[1024]{0:T(1024)S(1)} %pad_clamp_fusion.2), kind=kCustom, calls=%fused_computation.2 | custom fusion | bytes 8388736 | tf_op jit(solution)/shard_map/gather | solution.py:57
  110.5 2.8 %gather_fusion.3 = f32[32,2,32,512]{3,2,1,0:T(8,128)} fusion(f32[12,2,32,512]{3,2,1,0:T(8,128)S(1)} %copy.100, s32[1024]{0:T(1024)S(1)} %pad_clamp_fusion.1), kind=kCustom, calls=%fused_computation.3 | custom fusion | bytes 8388736 | tf_op jit(solution)/shard_map/gather | solution.py:56
  113.3 4.8 %fusion.10 = (f32[4,32,512]{2,1,0:T(8,128)S(1)}, f32[4,32,512]{2,1,0:T(8,128)S(1)}) fusion(f32[4,8,2,32,512]{4,3,2,1,0:T(8,128)} %bitcast.126, f32[4,8,2,32,512]{4,3,2,1,0:T(8,128)} %bitcast.127, f32[4,8]{1,0:T(4,128)S(1)} %fusion.29), kind=kLoop, calls=%fused_computation.29 | loop fusion | flops 5111808 | bytes 8913024 | tf_op jit(solution)/shard_map/reduce_sum | solution.py:61
  120.9 2.1 reshape.377
  123.0 3.7 %all-to-all-start = ((f32[8,1,16384]{2,1,0:T(1,128)}), f32[8,1,16384]{2,1,0:T(1,128)S(1)}, u32[]{:S(2)}, u32[]{:S(2)}) async-start(f32[8,1,16384]{2,1,0:T(1,128)} %reshape.377), calls=%async_computation | async-start | bytes 1048576 | tf_op jit(solution)/shard_map/all_to_all | solution.py:125
  127.7 13.0 %all-to-all-done = f32[8,1,16384]{2,1,0:T(1,128)S(1)} async-done(((f32[8,1,16384]{2,1,0:T(1,128)}), f32[8,1,16384]{2,1,0:T(1,128)S(1)}, u32[]{:S(2)}, u32[]{:S(2)}) %all-to-all-start) | async-done | bytes 524320 | tf_op jit(solution)/shard_map/all_to_all | solution.py:125
  141.2 2.7 %reduce = f32[8,16384]{1,0:T(8,128)} reduce(f32[8,1,16384]{2,1,0:T(1,128)S(1)} %all-to-all-done, f32[]{:T(128)} %broadcast.487), dimensions={1}, to_apply=%all_to_all.26.reduce_sub_computation | reduce | bytes 1048580 | tf_op jit(solution)/shard_map/all_to_all | solution.py:125
  151.5 5.5 %multiply_add_fusion = (f32[16,1,256,64]{2,3,1,0:T(8,128)S(1)}, f32[16,1,256,64]{2,3,1,0:T(8,128)S(1)}) fusion(f32[16,2,256,64]{2,3,1,0:T(8,128)} %gather_fusion.4, f32[256,64]{0,1:T(8,128)S(1)} %broadcast_add_fusion.1, f32[16]{0:T(128)S(1)} %get-tuple-element.32, f32[256,64]{0,1:T(8,128)S(1)} %copy-done.9, f32[16]{0:T(128)S(1)} %get-tuple-element.31, ...), kind=kLoop, calls=%fused_computation.37 | loop fusion | flops 3145728 | bytes 4391104 | tf_op jit(solution)/shard_map/add | solution.py:132
  157.0 2.8 %fusion.13 = f32[16,2,128,64]{2,3,1,0:T(8,128)} fusion(f32[16,1,256,64]{2,3,1,0:T(8,128)S(1)} %get-tuple-element.25, f32[16,1,256,64]{2,3,1,0:T(8,128)S(1)} %get-tuple-element.24, f32[256,128]{1,0:T(8,128)S(1)} %copy-done.10), kind=kOutput, calls=%fused_computation.33 | convolution fusion | flops 805830656 | bytes 3276800 | tf_op jit(solution)/shard_map/jt,ncjg->nctg/dot_general | solution.py:137
  159.8 3.3 %copy.108 = f32[16,2,128,64]{3,1,0,2:T(2,128)S(1)} copy(f32[16,2,128,64]{2,3,1,0:T(8,128)} %fusion.13) | data formatting | bytes 2097152 | tf_op jit(solution)/shard_map/jt,ncjg->nctg/transpose | solution.py:137
  163.2 3.0 %reshape.379 = f32[8,1,32768]{2,1,0:T(1,128)} reshape(f32[128,16,2,64]{3,2,1,0:T(2,128)S(1)} %bitcast.130) | data formatting | bytes 2097152
  166.2 4.4 %all-to-all-start.1 = ((f32[8,1,32768]{2,1,0:T(1,128)}), f32[8,1,32768]{2,1,0:T(1,128)}, u32[]{:S(2)}, u32[]{:S(2)}) async-start(f32[8,1,32768]{2,1,0:T(1,128)} %reshape.379), calls=%async_computation.1 | async-start | bytes 2097152 | tf_op jit(solution)/shard_map/all_to_all | solution.py:138
  170.6 2.1 collective-permute-start.1
  172.8 3.7 %collective-permute-start = (f32[16,2,16,256]{3,2,1,0:T(8,128)S(1)}, f32[16,2,16,256]{3,2,1,0:T(8,128)}, u32[]{:S(2)}, u32[]{:S(2)}) collective-permute-start(f32[16,2,16,256]{3,2,1,0:T(8,128)S(1)} %copy-done.6), channel_id=1, source_target_pairs={{0,8},{8,16},{16,24},{1,9},{9,17},{17,25},{2,10},{10,18},{18,26},{... | collective-permute-start | bytes 1572872 | tf_op jit(solution)/shard_map/ppermute | solution.py:19
  176.7 4.4 %gather_fusion = f32[256,2,16,256]{3,2,1,0:T(8,128)} fusion(f32[40,2,16,256]{3,2,1,0:T(8,128)S(1)} %copy-done, s32[1024]{0:T(1024)S(1)} %pad_clamp_fusion.4), kind=kCustom, calls=%fused_computation | custom fusion | bytes 16778240 | tf_op jit(solution)/shard_map/gather | solution.py:57
  183.7 4.4 %gather_fusion.1 = f32[256,2,16,256]{3,2,1,0:T(8,128)} fusion(f32[48,2,16,256]{3,2,1,0:T(8,128)S(1)} %pad_maximum_fusion.2, s32[1024]{0:T(1024)S(1)} %pad_clamp_fusion.3), kind=kCustom, calls=%fused_computation.1 | custom fusion | bytes 16778240 | tf_op jit(solution)/shard_map/gather | solution.py:56
  188.0 7.7 %fusion.3 = (f32[16,16,256]{2,1,0:T(8,128)}, f32[16,16,256]{2,1,0:T(8,128)}) fusion(f32[16,16,2,16,256]{4,3,2,1,0:T(8,128)} %bitcast.125, f32[16,16,2,16,256]{4,3,2,1,0:T(8,128)} %bitcast.124, f32[16,16]{1,0:T(8,128)S(1)} %fusion.26), kind=kLoop, calls=%fused_computation.11 | loop fusion | flops 10354688 | bytes 17302528 | tf_op jit(solution)/shard_map/reduce_sum | solution.py:61
  197.5 4.3 %reduce.1 = f32[8,32768]{1,0:T(8,128)S(1)} reduce(f32[8,1,32768]{2,1,0:T(1,128)} %all-to-all-done.1, f32[]{:T(128)} %broadcast.487), dimensions={1}, to_apply=%all_to_all.30.reduce_sub_computation | reduce | bytes 2097156 | tf_op jit(solution)/shard_map/all_to_all | solution.py:138
  206.9 3.3 %convolution_add_fusion = f32[16,2,16,256]{3,2,1,0:T(8,128)} fusion(f32[16,2,16,512]{3,2,1,0:T(8,128)} %all_to_all.33, f32[16,1,16,256]{3,2,1,0:T(8,128)} %bitcast.135, f32[16,1,16,256]{3,2,1,0:T(8,128)} %bitcast.134, f32[256,512]{1,0:T(8,128)} %param.17), kind=kOutput, calls=%fused_computation.35 | convolution fusion | flops 805568512 | bytes 2621440 | tf_op jit(solution)/shard_map/nctg,fg->nctf/dot_general | solution.py:139
  (87 shorter events, 30.5 us)
Async XLA Ops:
  7.2 169.5 %copy-start = (f32[40,2,16,256]{3,2,1,0:T(8,128)S(1)}, f32[40,2,16,256]{3,2,1,0:T(8,128)}, u32[]{:S(2)}) copy-start(f32[40,2,16,256]{3,2,1,0:T(8,128)} %param.18) | copy-start | bytes 3932164
  7.2 76.6 %all-gather.2.cloned.1.call-start = ((), (), s32[]{:S(2)}) async-start(), calls=%async_computation.2 | async-start | bytes 4718592 | tf_op jit(solution)/shard_map/all_gather | solution.py:108
  10.3 77.6 %copy-start.5 = (f32[256,512]{1,0:T(8,128)S(1)}, f32[256,512]{1,0:T(8,128)}, u32[]{:S(2)}) copy-start(f32[256,512]{1,0:T(8,128)} %param.17) | copy-start | bytes 1572868
  94.2 9.0 %copy-start.13 = (s32[4,8]{1,0:T(4,128)S(1)}, s32[4,8]{1,0:T(4,128)}, u32[]{:S(2)}) copy-start(s32[4,8]{1,0:T(4,128)} %param.25) | copy-start | bytes 388
  96.2 12.9 %copy-start.3 = (f32[4,2,32,512]{3,0,2,1:T(4,128)}, f32[4,2,32,512]{3,0,2,1:T(4,128)S(1)}, u32[]{:S(2)}) copy-start(f32[4,2,32,512]{3,0,2,1:T(4,128)S(1)} %fusion.11) | copy-start | bytes 1572868
  96.2 12.6 %collective-permute-start.3 = (f32[4,2,32,512]{3,0,2,1:T(4,128)S(1)}, f32[4,2,32,512]{3,0,2,1:T(4,128)S(1)}, u32[]{:S(2)}, u32[]{:S(2)}) collective-permute-start(f32[4,2,32,512]{3,0,2,1:T(4,128)S(1)} %fusion.11), channel_id=1, source_target_pairs={{8,0},{16,8},{24,16},{9,1},{17,9},{25,17},{10,2},{18,10},{26,18},{... | collective-permute-start | bytes 1572872 | tf_op jit(solution)/shard_map/ppermute | solution.py:20
  100.0 9.1 %collective-permute-start.2 = (f32[4,2,32,512]{3,0,2,1:T(4,128)S(1)}, f32[4,2,32,512]{3,0,2,1:T(4,128)S(1)}, u32[]{:S(2)}, u32[]{:S(2)}) collective-permute-start(f32[4,2,32,512]{3,0,2,1:T(4,128)S(1)} %fusion.11), channel_id=1, source_target_pairs={{0,8},{8,16},{16,24},{1,9},{9,17},{17,25},{2,10},{10,18},{18,26},{... | collective-permute-start | bytes 1572872 | tf_op jit(solution)/shard_map/ppermute | solution.py:19
  103.4 5.3 %copy-start.14 = (s32[4]{0:T(128)S(1)}, s32[4]{0:T(128)}, u32[]{:S(2)}) copy-start(s32[4]{0:T(128)} %param.27) | copy-start | bytes 52
  113.3 4.8 %copy-start.7 = (f32[4,2,32,512]{3,2,1,0:T(8,128)S(1)}, f32[4,2,32,512]{3,2,1,0:T(8,128)}, u32[]{:S(2)}) copy-start(f32[4,2,32,512]{3,2,1,0:T(8,128)} %param.15) | copy-start | bytes 1572868
  123.0 17.7 %all-to-all-start = ((f32[8,1,16384]{2,1,0:T(1,128)}), f32[8,1,16384]{2,1,0:T(1,128)S(1)}, u32[]{:S(2)}, u32[]{:S(2)}) async-start(f32[8,1,16384]{2,1,0:T(1,128)} %reshape.377), calls=%async_computation | async-start | bytes 1048576 | tf_op jit(solution)/shard_map/all_to_all | solution.py:125
  149.5 2.0 copy-start.9
  151.5 5.5 %copy-start.10 = (f32[256,128]{1,0:T(8,128)S(1)}, f32[256,128]{1,0:T(8,128)}, u32[]{:S(2)}) copy-start(f32[256,128]{1,0:T(8,128)} %param.16) | copy-start | bytes 393220
  163.1 13.3 %copy-start.11 = (s32[16,16]{1,0:T(8,128)S(1)}, s32[16,16]{1,0:T(8,128)}, u32[]{:S(2)}) copy-start(s32[16,16]{1,0:T(8,128)} %param.23) | copy-start | bytes 3076
  163.1 13.3 %copy-start.12 = (s32[16,16]{1,0:T(8,128)S(1)}, s32[16,16]{1,0:T(8,128)}, u32[]{:S(2)}) copy-start(s32[16,16]{1,0:T(8,128)} %param.22) | copy-start | bytes 3076
  166.2 4.4 %copy-start.6 = (f32[16,2,16,256]{3,2,1,0:T(8,128)S(1)}, f32[16,2,16,256]{3,2,1,0:T(8,128)}, u32[]{:S(2)}) copy-start(f32[16,2,16,256]{3,2,1,0:T(8,128)} %param.14) | copy-start | bytes 1572868
  166.2 31.3 %all-to-all-start.1 = ((f32[8,1,32768]{2,1,0:T(1,128)}), f32[8,1,32768]{2,1,0:T(1,128)}, u32[]{:S(2)}, u32[]{:S(2)}) async-start(f32[8,1,32768]{2,1,0:T(1,128)} %reshape.379), calls=%async_computation.1 | async-start | bytes 2097152 | tf_op jit(solution)/shard_map/all_to_all | solution.py:138
  170.6 10.9 %collective-permute-start.1 = (f32[16,2,16,256]{3,2,1,0:T(8,128)S(1)}, f32[16,2,16,256]{3,2,1,0:T(8,128)S(1)}, u32[]{:S(2)}, u32[]{:S(2)}) collective-permute-start(f32[16,2,16,256]{3,2,1,0:T(8,128)S(1)} %copy-done.6), channel_id=1, source_target_pairs={{8,0},{16,8},{24,16},{9,1},{17,9},{25,17},{10,2},{18,10},{26,18},{... | collective-permute-start | bytes 1572872 | tf_op jit(solution)/shard_map/ppermute | solution.py:20
  172.8 9.5 %collective-permute-start = (f32[16,2,16,256]{3,2,1,0:T(8,128)S(1)}, f32[16,2,16,256]{3,2,1,0:T(8,128)}, u32[]{:S(2)}, u32[]{:S(2)}) collective-permute-start(f32[16,2,16,256]{3,2,1,0:T(8,128)S(1)} %copy-done.6), channel_id=1, source_target_pairs={{0,8},{8,16},{16,24},{1,9},{9,17},{17,25},{2,10},{10,18},{18,26},{... | collective-permute-start | bytes 1572872 | tf_op jit(solution)/shard_map/ppermute | solution.py:19
  176.7 4.4 %copy-start.15 = (s32[16]{0:T(128)S(1)}, s32[16]{0:T(128)}, u32[]{:S(2)}) copy-start(s32[16]{0:T(128)} %param.24) | copy-start | bytes 196
  181.5 0.8 copy-start.8
  188.0 7.7 %copy-start.4 = (f32[4,2,32,512]{3,0,2,1:T(4,128)S(1)}, f32[4,2,32,512]{3,0,2,1:T(4,128)}, u32[]{:S(2)}) copy-start(f32[4,2,32,512]{3,0,2,1:T(4,128)} %copy-done.3) | copy-start | bytes 1572868
  188.0 8.6 %copy-start.2 = (f32[4,2,32,512]{3,2,0,1:T(8,128)S(1)}, f32[4,2,32,512]{3,2,0,1:T(8,128)}, u32[]{:S(2)}) copy-start(f32[4,2,32,512]{3,2,0,1:T(8,128)} %maximum_add_fusion) | copy-start | bytes 1572868
  205.4 4.8 %copy-start.1 = (f32[40,2,16,256]{3,2,1,0:T(8,128)S(1)}, f32[40,2,16,256]{3,2,1,0:T(8,128)}, u32[]{:S(2)}) copy-start(f32[40,2,16,256]{3,2,1,0:T(8,128)} %param.18) | copy-start | bytes 3932164
Sparse Core Ops, SparseCore 0:
  10.2 73.6 all-gather.1
where the time goes:
time: 218 us; the launch traced here: 217 us
  waiting for transfers between devices  88 us (40%)
  local copies, waits for them, and re-layouts  44.3 us (20%)
  other arithmetic  35.6 us (16%)
  starting transfers between devices  20.9 us (10%)
  between operations  14.4 us (7%)
  matrix products  13.9 us (6%)
    all_gather x1, waiting for transfers between devices, per_device(): lax.all_gather(child_rad, 'dir', axis=2, tiled=True)  73.6 us
    all_to_all x1, waiting for transfers between devices, per_device(): lax.all_to_all(parent_local, 'dir', split_axis=3, concat_axis=2, tiled=True)  13 us
    reduce_sum x2, other arithmetic, translate(): jnp.sum(live * (chosen[:, :, 0] * picked[:, :, 0] - chosen[:, :, 1] * pic...  12.4 us
    unnamed x38, local copies, waits for them, and re-layouts  11.5 us
    gather x2, local copies, waits for them, and re-layouts, translate(): chosen = operators[which_op]  9.64 us
    gather x2, local copies, waits for them, and re-layouts, translate(): picked = extended[position]  7.17 us
    ppermute x2, starting transfers between devices, extended_2(): before = lax.ppermute(last, axis, up)  6.86 us
    ppermute x2, starting transfers between devices, extended_2(): after = lax.ppermute(initial, axis, down)  5.94 us
  transfers between devices with their start and end apart: 7, of which 4 were waited for; matrix products, arithmetic and copies ran while one was open for 13% of the time, Pallas kernels for 0%

commit v1 on v0

v1 whole, which is shorter than its diff:
```python
import functools
import math

import jax
import jax.numpy as jnp
from jax import lax
from jax.experimental import pallas as pl
from jax.experimental.pallas import tpu as pltpu
from jax.sharding import PartitionSpec as P

phase_scale = 6.0
highest = lax.Precision.HIGHEST


def neighbours(array):
    size = lax.axis_size("box")
    up = [(i, i + 1) for i in range(size - 1)]
    down = [(i + 1, i) for i in range(size - 1)]
    return lax.ppermute(array, "box", up), lax.ppermute(array, "box", down)


def octant_signs(octant):
    first = 1.0 - 2.0 * (octant % 2).astype(jnp.float32)
    second = 1.0 - 2.0 * (octant // 2 % 2).astype(jnp.float32)
    third = 1.0 - 2.0 * (octant // 4 % 2).astype(jnp.float32)
    return (first, second, third)


def phase_block(octant, row_start, row_count, total_rows, col_start, col_count, total_cols):
    angle_rows = (row_start + jnp.arange(row_count, dtype=jnp.int32)).astype(jnp.float32)
    theta = math.pi * (angle_rows + 0.5) / total_rows
    angle_cols = (col_start + jnp.arange(col_count, dtype=jnp.int32)).astype(jnp.float32)
    azimuth = 2.0 * math.pi * angle_cols / total_cols
    sin_theta = jnp.sin(theta)[:, None]
    along_x = sin_theta * jnp.cos(azimuth)[None, :]
    along_y = sin_theta * jnp.sin(azimuth)[None, :]
    along_z = jnp.cos(theta)[:, None] + 0.0 * azimuth[None, :]
    first, second, third = octant_signs(octant)
    argument = phase_scale * (
        first[:, None, None] * along_x
        + second[:, None, None] * along_y
        + third[:, None, None] * along_z
    )
    return (jnp.cos(argument), jnp.sin(argument))


def exchange_body(count, matrix_ref, x_ref, *refs):
    if len(refs) == 7:
        extra_ref, out_ref, got, ready, landed, send_sem, recv_sem = refs
    else:
        out_ref, got, ready, landed, send_sem, recv_sem = refs
        extra_ref = None
    me = lax.axis_index("dir")
    planes, depth, width = got.shape[1:]
    rows = ready.shape[2]
    barrier = pltpu.get_barrier_semaphore()
    for step in range(1, count):
        pl.semaphore_signal(
            barrier,
            inc=1,
            device_id={"dir": lax.rem(me + step, count)},
            device_id_type=pl.DeviceIdType.MESH,
        )
    pl.semaphore_wait(barrier, count - 1)

    def push(source, target, leg):
        copies = []
        for step in range(1, count):
            peer = lax.rem(me + step, count)
            copy = pltpu.make_async_remote_copy(
                src_ref=source.at[peer],
                dst_ref=target.at[me],
                send_sem=send_sem.at[leg, step],
                recv_sem=recv_sem.at[leg, step],
                device_id={"dir": peer},
                device_id_type=pl.DeviceIdType.MESH,
            )
            copy.start()
            copies.append(copy)
        return copies

    def settle(target, leg):
        for step in range(1, count):
            origin = lax.rem(me + count - step, count)
            pltpu.make_async_remote_copy(
                src_ref=target.at[origin],
                dst_ref=target.at[origin],
                send_sem=send_sem.at[leg, step],
                recv_sem=recv_sem.at[leg, step],
                device_id={"dir": origin},
                device_id_type=pl.DeviceIdType.MESH,
            ).wait_recv()

    first = push(x_ref, got, 0)
    got[me] = x_ref[me]
    settle(got, 0)
    for plane in range(planes):
        product = jnp.dot(
            matrix_ref[...],
            got[:, plane].reshape(count * depth, width),
            precision=highest,
            preferred_element_type=jnp.float32,
        )
        ready[:, plane] = product.reshape(count, rows, width)
    second = push(ready, landed, 1)
    landed[me] = ready[me]
    settle(landed, 1)
    if extra_ref is None:
        out_ref[...] = landed[...]
    else:
        out_ref[...] = landed[...] + extra_ref[...]
    for copy in first + second:
        copy.wait_send()


def exchange(matrix, x, extra, which):
    count, planes, depth, width = x.shape
    rows = matrix.shape[0] // count
    operands = (matrix, x) if extra is None else (matrix, x, extra)
    return pl.pallas_call(
        functools.partial(exchange_body, count),
        out_shape=jax.ShapeDtypeStruct((count, planes, rows, width), jnp.float32),
        in_specs=[pl.BlockSpec(memory_space=pltpu.VMEM)] * len(operands),
        out_specs=pl.BlockSpec(memory_space=pltpu.VMEM),
        scratch_shapes=[
            pltpu.VMEM((count, planes, depth, width), jnp.float32),
            pltpu.VMEM((count, planes, rows, width), jnp.float32),
            pltpu.VMEM((count, planes, rows, width), jnp.float32),
            pltpu.SemaphoreType.DMA((2, count)),
            pltpu.SemaphoreType.DMA((2, count)),
        ],
        compiler_params=pltpu.CompilerParams(collective_id=which, has_side_effects=True),
        name="exchange_" + str(which),
    )(*operands)


def translate_body(has_base, *refs):
    source_ref, which_ref, length_ref, before, own, after, ops_ref = refs[:7]
    base_ref = refs[7] if has_base else None
    out_ref, wide, sems = refs[-3:]
    boxes, _, rows, width = own.shape
    copies = [
        pltpu.make_async_copy(part, wide.at[pl.ds(at * boxes, boxes)], sems.at[at])
        for at, part in enumerate((before, own, after))
    ]
    for copy in copies:
        copy.start()
    for copy in copies:
        copy.wait()
    offset = (lax.axis_index("box") - 1) * boxes
    tall = rows
    while tall % 16 == 0 and tall * width > 4096:
        tall //= 2

    def one_box(box, carry):
        length = length_ref[box]
        for start in range(0, rows, tall):
            part = slice(start, start + tall)

            def entry(column, totals):
                real, imag = totals
                at = source_ref[box, column] - offset
                op = which_ref[box, column]
                op_real, op_imag = ops_ref[op, 0, part], ops_ref[op, 1, part]
                re, im = wide[at, 0, part], wide[at, 1, part]
                real = real + (op_real * re - op_imag * im)
                imag = imag + (op_real * im + op_imag * re)
                return real, imag

            if has_base:
                initial = (base_ref[box, 0, part], base_ref[box, 1, part])
            else:
                initial = (jnp.zeros((tall, width), jnp.float32),) * 2
            real, imag = lax.fori_loop(0, length, entry, initial)
            out_ref[box, 0, part] = real
            out_ref[box, 1, part] = imag
        return carry

    lax.fori_loop(0, boxes, one_box, 0)


def translate(own, before, after, operators, source, which_op, length, base, name):
    boxes = own.shape[0]
    vmem = pl.BlockSpec(memory_space=pltpu.VMEM)
    smem = pl.BlockSpec(memory_space=pltpu.SMEM)
    anywhere = pl.BlockSpec(memory_space=pl.ANY)
    operands = [source, which_op, length, before, own, after, operators]
    specs = [smem] * 3 + [anywhere] * 3 + [vmem]
    if base is not None:
        operands.append(base)
        specs.append(vmem)
    return pl.pallas_call(
        functools.partial(translate_body, base is not None),
        out_shape=jax.ShapeDtypeStruct(own.shape, jnp.float32),
        in_specs=specs,
        out_specs=vmem,
        scratch_shapes=[
            pltpu.VMEM((3 * boxes,) + own.shape[1:], jnp.float32),
            pltpu.SemaphoreType.DMA((3,)),
        ],
        compiler_params=pltpu.CompilerParams(vmem_limit_bytes=40 * 1024 * 1024),
        name=name,
    )(*operands)


def per_device(
    child_rad,
    parent_incoming,
    theta_interp,
    phi_interp,
    child_ops,
    parent_ops,
    child_parent,
    child_octant,
    far_child_src,
    far_child_op,
    far_child_len,
    far_parent_src,
    far_parent_op,
    far_parent_len,
):
    child_count, _, theta_child, phi_child = child_rad.shape
    parent_count, _, theta_parent, phi_parent = parent_incoming.shape
    theta_total = theta_interp.shape[0]
    dir_count = lax.axis_size("dir")
    planes = child_count * 2 // dir_count
    padded = -(-theta_child // 8) * 8
    box_index = lax.axis_index("box")
    dir_index = lax.axis_index("dir")
    parent_slot = child_parent - box_index * parent_count
    member = (parent_slot[None, :] == jnp.arange(parent_count, dtype=jnp.int32)[:, None]).astype(
        jnp.float32
    )
    grow = ((0, 0), (0, 0), (0, padded - theta_child), (0, 0))
    spread = jnp.pad(
        theta_interp.reshape(theta_total, dir_count, theta_child),
        ((0, 0), (0, 0), (0, padded - theta_child)),
    ).reshape(theta_total, dir_count * padded)
    before, after = neighbours(child_rad)
    theta_done = exchange(
        spread, jnp.pad(child_rad, grow).reshape(dir_count, planes, padded, phi_child), None, 0
    )
    child_trans = translate(
        child_rad, before, after, child_ops, far_child_src, far_child_op, far_child_len, None,
        "child_translate",
    )
    theta_done = theta_done.reshape(child_count, 2, theta_parent, phi_child)
    interp = jnp.einsum("ncjf,fg->ncjg", theta_done, phi_interp, precision=highest)
    cosine, sine = phase_block(
        jnp.arange(8, dtype=jnp.int32), dir_index * theta_parent, theta_parent, theta_total,
        0, phi_parent, phi_parent,
    )
    cosine, sine = lax.optimization_barrier((cosine, sine))
    cosine, sine = cosine[child_octant], sine[child_octant]
    shifted = jnp.stack(
        [cosine * interp[:, 0] - sine * interp[:, 1], sine * interp[:, 0] + cosine * interp[:, 1]],
        axis=1,
    )
    parent_rad = jnp.einsum("pn,ncjg->pcjg", member, shifted, precision=highest)
    before, after = neighbours(parent_rad)
    parent_local = translate(
        parent_rad, before, after, parent_ops, far_parent_src, far_parent_op, far_parent_len,
        parent_incoming, "parent_translate",
    )
    own_field = parent_local[parent_slot]
    unshift = jnp.stack(
        [
            cosine * own_field[:, 0] + sine * own_field[:, 1],
            cosine * own_field[:, 1] - sine * own_field[:, 0],
        ],
        axis=1,
    )
    back_phi = jnp.einsum("ncjg,fg->ncjf", unshift, phi_interp, precision=highest)
    extra = jnp.pad(child_trans, grow).reshape(dir_count, planes, padded, phi_child)
    child_local = exchange(
        spread.T, back_phi.reshape(dir_count, planes, theta_parent, phi_child), extra, 1
    )
    child_local = child_local.reshape(child_count, 2, padded, phi_child)[:, :, :theta_child]
    return (child_local, parent_local, parent_rad)


def solution(mesh):
    in_specs = (
        P("box", None, "dir", None),
        P("box", None, "dir", None),
        P(),
        P(),
        P(None, None, "dir", None),
        P(None, None, "dir", None),
        P("box"),
        P("box"),
        P("box", None),
        P("box", None),
        P("box"),
        P("box", None),
        P("box", None),
        P("box"),
    )
    out_specs = (
        P("box", None, "dir", None),
        P("box", None, "dir", None),
        P("box", None, "dir", None),
    )
    return jax.shard_map(
        per_device, mesh=mesh, in_specs=in_specs, out_specs=out_specs, check_vma=False
    )
```

time: 218 us -> 138 us (0.63)
  Pallas kernels: 0 us -> 91.2 us
  waiting for transfers between devices: 88 us -> 2.03 us
  local copies, waits for them, and re-layouts: 44.3 us -> 10.5 us
  other arithmetic: 35.6 us -> 7.32 us
  between operations: 14.4 us -> 1.02 us
  starting transfers between devices: 20.9 us -> 14.4 us
  matrix products: 13.9 us -> 9.44 us
    pallas_call x0 -> x4, Pallas kernels: none -> 91.2 us  [the longest x2 84.6 us: exchange(): pl.pallas_call(functools.partial(exchange_body, count), out_shape=jax.Sha...]
    all_gather x1 -> x0, waiting for transfers between devices: 73.6 us -> none  [per_device(): lax.all_gather(child_rad, 'dir', axis=2, tiled=True)]
    gather x5 -> x3, local copies, waits for them, and re-layouts: 18.8 us -> 4.38 us  [the longest x1 3.15 us: per_device(): own_field = parent_local[parent_slot]]
    all_to_all x2 -> x0, waiting for transfers between devices: 13 us -> none  [the longest x1 13 us: per_device(): lax.all_to_all(parent_local, 'dir', split_axis=3, concat_axis=2, tiled=True)]
    reduce_sum x2 -> x0, other arithmetic: 12.4 us -> none  [translate(): jnp.sum(live * (chosen[:, :, 0] * picked[:, :, 0] - chosen[:, :, 1] * pic...]
    all_to_all x2 -> x0, starting transfers between devices: 8.09 us -> none  [the longest x1 4.37 us: per_device(): lax.all_to_all(back_cols, 'dir', split_axis=2, concat_axis=3, tiled=True)]
    all_to_all x6 -> x0, local copies, waits for them, and re-layouts: 7.42 us -> none  [the longest x3 3.85 us: per_device(): lax.all_to_all(parent_local, 'dir', split_axis=3, concat_axis=2, tiled=True)]
    dot_general x3 -> x1, matrix products: 10.1 us -> 2.83 us  [per_device(): jnp.einsum('ncjg,fg->ncjf', unshift, phi_interp, precision=highest)]
  transfers between devices with their start and end apart: 7 -> 4, of which waited for: 4 -> 1; matrix products, arithmetic and copies ran while one was open for 13% -> 7% of each run, Pallas kernels for 0% -> 2%
where the time goes in v1:
time: 138 us; the launch traced here: 136 us
  Pallas kernels  91.2 us (66%)
  starting transfers between devices  14.4 us (10%)
  local copies, waits for them, and re-layouts  10.5 us (8%)
  matrix products  9.44 us (7%)
  other arithmetic  7.32 us (5%)
  waiting for transfers between devices  2.03 us (1%)
    pallas_call x2, Pallas kernels, exchange(): pl.pallas_call(functools.partial(exchange_body, count), out_shape=jax.Sha...  84.6 us
    ppermute x4, starting transfers between devices, neighbours(): return (lax.ppermute(array, 'box', up), lax.ppermute(array, 'box', down))  14.4 us
    pallas_call x2, Pallas kernels, translate(): pl.pallas_call(functools.partial(translate_body, base is not None), out_s...  6.55 us
    unnamed x38, local copies, waits for them, and re-layouts  5.99 us
    dot_general x1, matrix products, per_device(): parent_rad = jnp.einsum('pn,ncjg->pcjg', member, shifted, precision=highest)  3.55 us
    gather x1, local copies, waits for them, and re-layouts, per_device(): own_field = parent_local[parent_slot]  3.15 us
    dot_general x1, matrix products, per_device(): jnp.einsum('ncjf,fg->ncjg', theta_done, phi_interp, precision=highest)  3.06 us
    dot_general x1, matrix products, per_device(): jnp.einsum('ncjg,fg->ncjf', unshift, phi_interp, precision=highest)  2.83 us
  transfers between devices with their start and end apart: 4, of which 1 were waited for; matrix products, arithmetic and copies ran while one was open for 7% of the time, Pallas kernels for 2%

profile of v1, /device:TPU:1, one launch (start us, length us, event | category | flops | bytes accessed | tf_op | source)
XLA Modules:
  0.0 135.9 jit_solution(12021255012245270056)
XLA Ops:
  0.9 2.0 %fusion.13 = (f32[8,32,512]{2,1,0:T(8,128)S(1)}, f32[8,32,512]{2,1,0:T(8,128)S(1)}) fusion(f32[32,512]{1,0:T(8,128)S(1)} %broadcast_add_fusion, f32[8]{0:T(128)S(1)} %fusion.28, f32[32,512]{1,0:T(8,128)S(1)} %get-tuple-element.19, f32[8]{0:T(128)S(1)} %get-tuple-element.25, f32[32,512]{1,0:T(8,128)S(1)} %get-tuple-element.18, f32[8]{0:T(128)S(1)} %get-tuple-element.24), kind=kLoop, calls=%fused_computation.26 | loop fusion | flops 786432 | bytes 1245280 | tf_op jit(solution)/shard_map/sin | solution.py:44
  3.0 0.7 compare_select_fusion.1
  3.6 0.6 gather_fusion
  4.3 0.6 gather_fusion.1
  4.9 34.7 %exchange_0.1 = f32[8,4,32,256]{3,2,1,0:T(8,128)} custom-call(f32[256,128]{1,0:T(8,128)} %matrix_ref.1, f32[8,4,16,256]{3,2,1,0:T(8,128)} %bitcast.46), custom_call_target="tpu_custom_call" | custom-call | tf_op jit(solution)/shard_map/exchange_0/pallas_call | solution.py:120
  39.6 3.1 %fusion.11 = f32[16,2,32,512]{3,2,1,0:T(8,128)S(1)} fusion(f32[16,2,32,256]{3,2,1,0:T(8,128)} %bitcast.48, f32[256,512]{1,0:T(8,128)S(1)} %copy-done), kind=kOutput, calls=%fused_computation.23 | convolution fusion | flops 1610612736 | bytes 3670016 | tf_op jit(solution)/shard_map/ncjf,fg->ncjg/dot_general | solution.py:248
  42.7 0.5 fusion.6
  43.2 1.5 %pad_maximum_fusion = f32[16,2,32,512]{3,2,1,0:T(8,128)} fusion(f32[16,1,32,512]{3,2,1,0:T(8,128)S(1)} %get-tuple-element.15, f32[16,1,32,512]{3,2,1,0:T(8,128)S(1)} %get-tuple-element.14), kind=kLoop, calls=%fused_computation.3 | loop fusion | flops 524288 | bytes 4194304 | tf_op jit(solution)/shard_map/stack | solution.py:255
  44.8 3.5 %fusion.4 = f32[4,2,32,512]{3,0,2,1:T(4,128)S(1)} fusion(f32[16,2,32,512]{3,2,1,0:T(8,128)} %pad_maximum_fusion, s32[16]{0:T(128)S(1)} %get-tuple-element.11), kind=kOutput, calls=%fused_computation.8 | convolution fusion | flops 25165888 | bytes 2621504 | tf_op jit(solution)/shard_map/pn,ncjg->pcjg/dot_general | solution.py:259
  48.5 6.8 %collective-permute-start = (f32[4,2,32,512]{3,2,1,0:T(8,128)S(1)}, f32[4,2,32,512]{3,2,1,0:T(8,128)S(1)}, u32[]{:S(2)}, u32[]{:S(2)}) collective-permute-start(f32[4,2,32,512]{3,2,1,0:T(8,128)S(1)} %copy.19.refs_4_), channel_id=1, source_target_pairs={{0,8},{8,16},{16,24},{1,9},{9,17},{17,25},{2,10},{10,18},{18,26},{... | collective-permute-start | bytes 1572872 | tf_op jit(solution)/shard_map/ppermute | solution.py:19
  55.3 1.9 %collective-permute-start.1 = (f32[4,2,32,512]{3,2,1,0:T(8,128)S(1)}, f32[4,2,32,512]{3,2,1,0:T(8,128)S(1)}, u32[]{:S(2)}, u32[]{:S(2)}) collective-permute-start(f32[4,2,32,512]{3,2,1,0:T(8,128)S(1)} %copy.19.refs_4_), channel_id=1, source_target_pairs={{8,0},{16,8},{24,16},{9,1},{17,9},{25,17},{10,2},{18,10},{26,18},{... | collective-permute-start | bytes 1572872 | tf_op jit(solution)/shard_map/ppermute | solution.py:19
  57.2 3.6 %collective-permute-start.2 = (f32[16,2,16,256]{3,2,1,0:T(8,128)S(1)}, f32[16,2,16,256]{3,2,1,0:T(8,128)}, u32[]{:S(2)}, u32[]{:S(2)}) collective-permute-start(f32[16,2,16,256]{3,2,1,0:T(8,128)S(1)} %copy-done.4), channel_id=1, source_target_pairs={{0,8},{8,16},{16,24},{1,9},{9,17},{17,25},{2,10},{10,18},{18,26},{... | collective-permute-start | bytes 1572872 | tf_op jit(solution)/shard_map/ppermute | solution.py:19
  60.9 2.1 %collective-permute-start.3 = (f32[16,2,16,256]{3,2,1,0:T(8,128)S(1)}, f32[16,2,16,256]{3,2,1,0:T(8,128)}, u32[]{:S(2)}, u32[]{:S(2)}) collective-permute-start(f32[16,2,16,256]{3,2,1,0:T(8,128)S(1)} %copy-done.4), channel_id=1, source_target_pairs={{8,0},{16,8},{24,16},{9,1},{17,9},{25,17},{10,2},{18,10},{26,18},{... | collective-permute-start | bytes 1572872 | tf_op jit(solution)/shard_map/ppermute | solution.py:19
  63.0 0.8 copy.17
  63.7 2.0 %collective-permute-done.1.refs_5_ = f32[4,2,32,512]{3,2,1,0:T(8,128)S(1)} collective-permute-done((f32[4,2,32,512]{3,2,1,0:T(8,128)S(1)}, f32[4,2,32,512]{3,2,1,0:T(8,128)S(1)}, u32[]{:S(2)}, u32[]{:S(2)}) %collective-permute-start.1) | collective-permute-done | bytes 524320 | tf_op jit(solution)/shard_map/ppermute | solution.py:19
  65.8 2.5 %copy-done.1 = f32[40,2,32,512]{3,2,1,0:T(8,128)S(1)} copy-done((f32[40,2,32,512]{3,2,1,0:T(8,128)S(1)}, f32[40,2,32,512]{3,2,1,0:T(8,128)}, u32[]{:S(2)}) %copy-start.1) | copy-done | bytes 5242904
  68.3 2.4 %parent_translate.1 = f32[4,2,32,512]{3,2,1,0:T(8,128)} custom-call(s32[4,8]{1,0:T(4,128)S(1)} %copy-done.9, s32[4,8]{1,0:T(4,128)S(1)} %copy-done.10, s32[4]{0:T(128)S(1)} %copy-done.11, f32[4,2,32,512]{3,2,1,0:T(8,128)S(1)} %collective-permute-done.refs_3_, f32[4,2,32,512]{3,2,1,0:T(8,128)S(1)} %copy.19.refs_4_, ...), custom_call_target="tpu_custom_call" | custom-call | tf_op jit(solution)/shard_map/parent_translate/pallas_call | solution.py:192
  70.7 3.1 %gather_fusion.2 = f32[16,2,32,512]{3,2,1,0:T(8,128)} fusion(f32[4,2,32,512]{3,2,1,0:T(8,128)} %parent_translate.1, s32[1024]{0:T(1024)S(1)} %pad_clamp_fusion), kind=kCustom, calls=%fused_computation.2 | custom fusion | bytes 4194368 | tf_op jit(solution)/shard_map/gather | solution.py:265
  73.9 2.4 %fusion.8 = (f32[16,1,32,512]{3,2,1,0:T(8,128)S(1)}, f32[16,1,32,512]{3,2,1,0:T(8,128)S(1)}) fusion(f32[16,32,512]{2,1,0:T(8,128)} %copy-done.15, f32[16,32,512]{2,1,0:T(8,128)S(1)} %copy-done.14, f32[16,2,32,512]{3,2,1,0:T(8,128)} %gather_fusion.2), kind=kLoop, calls=%fused_computation.16 | loop fusion | flops 1572864 | bytes 6291456 | tf_op jit(solution)/shard_map/add | solution.py:268
  76.3 2.8 %fusion = f32[16,2,32,256]{3,2,1,0:T(8,128)} fusion(f32[16,1,32,512]{3,2,1,0:T(8,128)S(1)} %get-tuple-element.13, f32[16,1,32,512]{3,2,1,0:T(8,128)S(1)} %get-tuple-element.12, f32[256,512]{1,0:T(8,128)S(1)} %copy-done), kind=kOutput, calls=%fused_computation.4 | convolution fusion | flops 1611137024 | bytes 3670016 | tf_op jit(solution)/shard_map/ncjg,fg->ncjf/dot_general | solution.py:273
  79.1 4.2 %child_translate.1 = f32[16,2,16,256]{3,2,1,0:T(8,128)S(1)} custom-call(s32[16,16]{1,0:T(8,128)S(1)} %copy-done.7, s32[16,16]{1,0:T(8,128)S(1)} %copy-done.8, s32[16]{0:T(128)S(1)} %copy-done.12, f32[16,2,16,256]{3,2,1,0:T(8,128)} %collective-permute-done.2.refs_3_, f32[16,2,16,256]{3,2,1,0:T(8,128)S(1)} %copy-done.4, ...), custom_call_target="tpu_custom_call" | custom-call | tf_op jit(solution)/shard_map/child_translate/pallas_call | solution.py:192
  83.3 0.8 copy-done.3
  84.1 50.0 %exchange_1.1 = f32[8,4,16,256]{3,2,1,0:T(8,128)} custom-call(f32[128,256]{1,0:T(8,128)} %bitcast.50, f32[8,4,32,256]{3,2,1,0:T(8,128)} %bitcast.47, f32[8,4,16,256]{3,2,1,0:T(8,128)} %bitcast.45), custom_call_target="tpu_custom_call" | custom-call | tf_op jit(solution)/shard_map/exchange_1/pallas_call | solution.py:120
  134.1 1.9 %copy.28 = f32[16,2,16,256]{3,2,1,0:T(8,128)} copy(f32[16,2,16,256]{3,2,1,0:T(8,128)} %bitcast.49) | data formatting | bytes 1048576
  (48 shorter events, 0.6 us)
Async XLA Ops:
  0.6 38.9 %copy-start = (f32[256,512]{1,0:T(8,128)S(1)}, f32[256,512]{1,0:T(8,128)}, u32[]{:S(2)}) copy-start(f32[256,512]{1,0:T(8,128)} %param.17) | copy-start | bytes 1572868
  4.3 38.4 %copy-start.13 = (f32[16,32,512]{2,1,0:T(8,128)}, f32[16,32,512]{2,1,0:T(8,128)S(1)}, u32[]{:S(2)}) copy-start(f32[16,32,512]{2,1,0:T(8,128)S(1)} %gather_fusion) | copy-start | bytes 3145732
  4.9 37.8 %copy-start.15 = (f32[16,32,512]{2,1,0:T(8,128)}, f32[16,32,512]{2,1,0:T(8,128)S(1)}, u32[]{:S(2)}) copy-start(f32[16,32,512]{2,1,0:T(8,128)S(1)} %gather_fusion.1) | copy-start | bytes 3145732
  43.2 1.6 %copy-start.17 = (s32[16]{0:T(128)S(1)}, s32[16]{0:T(128)}, u32[]{:S(2)}) copy-start(s32[16]{0:T(128)} %param.20) | copy-start | bytes 196
  44.7 12.5 %copy-start.4 = (f32[16,2,16,256]{3,2,1,0:T(8,128)S(1)}, f32[16,2,16,256]{3,2,1,0:T(8,128)}, u32[]{:S(2)}) copy-start(f32[16,2,16,256]{3,2,1,0:T(8,128)} %refs_4_.1) | copy-start | bytes 1572868
  44.7 18.3 %copy-start.16 = (f32[256,128]{1,0:T(8,128)S(1)}, f32[256,128]{1,0:T(8,128)}, u32[]{:S(2)}) copy-start(f32[256,128]{1,0:T(8,128)} %matrix_ref.1) | copy-start | bytes 393220
  44.7 21.1 %copy-start.6 = (f32[4,2,32,512]{3,2,1,0:T(8,128)S(1)}, f32[4,2,32,512]{3,2,1,0:T(8,128)}, u32[]{:S(2)}) copy-start(f32[4,2,32,512]{3,2,1,0:T(8,128)} %refs_7_.1) | copy-start | bytes 1572868
  44.7 21.1 %copy-start.9 = (s32[4,8]{1,0:T(4,128)S(1)}, s32[4,8]{1,0:T(4,128)}, u32[]{:S(2)}) copy-start(s32[4,8]{1,0:T(4,128)} %refs_0_.2) | copy-start | bytes 388
  44.7 21.1 %copy-start.10 = (s32[4,8]{1,0:T(4,128)S(1)}, s32[4,8]{1,0:T(4,128)}, u32[]{:S(2)}) copy-start(s32[4,8]{1,0:T(4,128)} %refs_1_.2) | copy-start | bytes 388
  44.7 21.1 %copy-start.11 = (s32[4]{0:T(128)S(1)}, s32[4]{0:T(128)}, u32[]{:S(2)}) copy-start(s32[4]{0:T(128)} %refs_2_.2) | copy-start | bytes 52
  48.5 22.2 %copy-start.2 = (f32[4,2,32,512]{3,2,1,0:T(8,128)}, f32[4,2,32,512]{3,2,1,0:T(8,128)S(1)}, u32[]{:S(2)}) copy-start(f32[4,2,32,512]{3,2,1,0:T(8,128)S(1)} %copy.19.refs_4_) | copy-start | bytes 1572868
  48.5 15.2 %collective-permute-start = (f32[4,2,32,512]{3,2,1,0:T(8,128)S(1)}, f32[4,2,32,512]{3,2,1,0:T(8,128)S(1)}, u32[]{:S(2)}, u32[]{:S(2)}) collective-permute-start(f32[4,2,32,512]{3,2,1,0:T(8,128)S(1)} %copy.19.refs_4_), channel_id=1, source_target_pairs={{0,8},{8,16},{16,24},{1,9},{9,17},{17,25},{2,10},{10,18},{18,26},{... | collective-permute-start | bytes 1572872 | tf_op jit(solution)/shard_map/ppermute | solution.py:19
  55.3 10.5 %collective-permute-start.1 = (f32[4,2,32,512]{3,2,1,0:T(8,128)S(1)}, f32[4,2,32,512]{3,2,1,0:T(8,128)S(1)}, u32[]{:S(2)}, u32[]{:S(2)}) collective-permute-start(f32[4,2,32,512]{3,2,1,0:T(8,128)S(1)} %copy.19.refs_4_), channel_id=1, source_target_pairs={{8,0},{16,8},{24,16},{9,1},{17,9},{25,17},{10,2},{18,10},{26,18},{... | collective-permute-start | bytes 1572872 | tf_op jit(solution)/shard_map/ppermute | solution.py:19
  57.2 21.9 %collective-permute-start.2 = (f32[16,2,16,256]{3,2,1,0:T(8,128)S(1)}, f32[16,2,16,256]{3,2,1,0:T(8,128)}, u32[]{:S(2)}, u32[]{:S(2)}) collective-permute-start(f32[16,2,16,256]{3,2,1,0:T(8,128)S(1)} %copy-done.4), channel_id=1, source_target_pairs={{0,8},{8,16},{16,24},{1,9},{9,17},{17,25},{2,10},{10,18},{18,26},{... | collective-permute-start | bytes 1572872 | tf_op jit(solution)/shard_map/ppermute | solution.py:19
  60.9 18.2 %collective-permute-start.3 = (f32[16,2,16,256]{3,2,1,0:T(8,128)S(1)}, f32[16,2,16,256]{3,2,1,0:T(8,128)}, u32[]{:S(2)}, u32[]{:S(2)}) collective-permute-start(f32[16,2,16,256]{3,2,1,0:T(8,128)S(1)} %copy-done.4), channel_id=1, source_target_pairs={{8,0},{16,8},{24,16},{9,1},{17,9},{25,17},{10,2},{18,10},{26,18},{... | collective-permute-start | bytes 1572872 | tf_op jit(solution)/shard_map/ppermute | solution.py:19
  65.8 2.5 %copy-start.1 = (f32[40,2,32,512]{3,2,1,0:T(8,128)S(1)}, f32[40,2,32,512]{3,2,1,0:T(8,128)}, u32[]{:S(2)}) copy-start(f32[40,2,32,512]{3,2,1,0:T(8,128)} %refs_6_.2) | copy-start | bytes 15728644
  70.7 3.2 %copy-start.14 = (f32[16,32,512]{2,1,0:T(8,128)S(1)}, f32[16,32,512]{2,1,0:T(8,128)}, u32[]{:S(2)}) copy-start(f32[16,32,512]{2,1,0:T(8,128)} %copy-done.13) | copy-start | bytes 3145732
  76.2 2.9 %copy-start.5 = (f32[40,2,16,256]{3,2,1,0:T(8,128)S(1)}, f32[40,2,16,256]{3,2,1,0:T(8,128)}, u32[]{:S(2)}) copy-start(f32[40,2,16,256]{3,2,1,0:T(8,128)} %refs_6_.3) | copy-start | bytes 3932164
  76.2 2.9 %copy-start.7 = (s32[16,16]{1,0:T(8,128)S(1)}, s32[16,16]{1,0:T(8,128)}, u32[]{:S(2)}) copy-start(s32[16,16]{1,0:T(8,128)} %refs_0_.3) | copy-start | bytes 3076
  76.2 2.9 %copy-start.8 = (s32[16,16]{1,0:T(8,128)S(1)}, s32[16,16]{1,0:T(8,128)}, u32[]{:S(2)}) copy-start(s32[16,16]{1,0:T(8,128)} %refs_1_.3) | copy-start | bytes 3076
  76.3 2.9 %copy-start.12 = (s32[16]{0:T(128)S(1)}, s32[16]{0:T(128)}, u32[]{:S(2)}) copy-start(s32[16]{0:T(128)} %refs_2_.3) | copy-start | bytes 196
  83.3 0.8 copy-start.3

commit v2 on v1

--- a/solution.py
+++ b/solution.py
@@ -44,57 +44,98 @@
     return (jnp.cos(argument), jnp.sin(argument))
 
 
-def exchange_body(count, matrix_ref, x_ref, *refs):
-    if len(refs) == 7:
-        extra_ref, out_ref, got, ready, landed, send_sem, recv_sem = refs
-    else:
-        out_ref, got, ready, landed, send_sem, recv_sem = refs
-        extra_ref = None
+def flipped(index, mask):
+    result = index
+    bit = 1
+    while bit <= mask:
+        if mask & bit:
+            result = result + bit - 2 * bit * lax.rem(lax.div(index, bit), 2)
+        bit *= 2
+    return result
+
+
+def exchange_body(count, around, fields, matrix_ref, x_ref, *refs):
+    refs = list(refs)
+    extra_ref = None if around else refs.pop(0)
+    out_ref = refs.pop(0)
+    if around:
+        below_ref, above_ref = refs.pop(0), refs.pop(0)
+    got, ready, landed, send_sem, recv_sem = refs[:5]
     me = lax.axis_index("dir")
     planes, depth, width = got.shape[1:]
     rows = ready.shape[2]
+    mesh_ids = pl.DeviceIdType.MESH
     barrier = pltpu.get_barrier_semaphore()
-    for step in range(1, count):
+    steps = range(count - 1, 0, -1)
+
+    def partner(step):
+        if count & (count - 1):
+            return lax.rem(me + step, count), lax.rem(me + count - step, count)
+        peer = flipped(me, step)
+        return peer, peer
+
+    for step in steps:
         pl.semaphore_signal(
-            barrier,
-            inc=1,
-            device_id={"dir": lax.rem(me + step, count)},
-            device_id_type=pl.DeviceIdType.MESH,
+            barrier, inc=1, device_id={"dir": partner(step)[0]}, device_id_type=mesh_ids
         )
-    pl.semaphore_wait(barrier, count - 1)
-
-    def push(source, target, leg):
-        copies = []
-        for step in range(1, count):
-            peer = lax.rem(me + step, count)
+    greeted = count - 1
+    if around:
+        box = lax.axis_index("box")
+        upper = lax.rem(box + 1, fields)
+        lower = lax.rem(box + fields - 1, fields)
+        for other in (upper, lower):
+            pl.semaphore_signal(
+                barrier, inc=1, device_id={"box": other}, device_id_type=mesh_ids
+            )
+        greeted += 2
+    pl.semaphore_wait(barrier, greeted)
+
+    def push(source, target, leg, plane):
+        for step in steps:
+            peer, _ = partner(step)
             copy = pltpu.make_async_remote_copy(
-                src_ref=source.at[peer],
-                dst_ref=target.at[me],
-                send_sem=send_sem.at[leg, step],
-                recv_sem=recv_sem.at[leg, step],
+                src_ref=source.at[peer, plane],
+                dst_ref=target.at[me, plane],
+                send_sem=send_sem.at[leg, plane, step],
+                recv_sem=recv_sem.at[leg, plane, step],
                 device_id={"dir": peer},
-                device_id_type=pl.DeviceIdType.MESH,
+                device_id_type=mesh_ids,
             )
             copy.start()
-            copies.append(copy)
-        return copies
-
-    def settle(target, leg):
-        for step in range(1, count):
-            origin = lax.rem(me + count - step, count)
+            started.append(copy)
+
+    def settle(target, leg, plane):
+        for step in steps:
+            _, origin = partner(step)
             pltpu.make_async_remote_copy(
-                src_ref=target.at[origin],
-                dst_ref=target.at[origin],
-                send_sem=send_sem.at[leg, step],
-                recv_sem=recv_sem.at[leg, step],
+                src_ref=target.at[origin, plane],
+                dst_ref=target.at[origin, plane],
+                send_sem=send_sem.at[leg, plane, step],
+                recv_sem=recv_sem.at[leg, plane, step],
                 device_id={"dir": origin},
-                device_id_type=pl.DeviceIdType.MESH,
+                device_id_type=mesh_ids,
             ).wait_recv()
 
-    first = push(x_ref, got, 0)
+    started = []
+    for plane in range(planes):
+        push(x_ref, got, 0, plane)
+    ring = []
+    if around:
+        box_send, box_recv = refs[5:7]
+        for at, (other, target) in enumerate(((upper, below_ref), (lower, above_ref))):
+            copy = pltpu.make_async_remote_copy(
+                src_ref=x_ref,
+                dst_ref=target,
+                send_sem=box_send.at[at],
+                recv_sem=box_recv.at[at],
+                device_id={"box": other},
+                device_id_type=mesh_ids,
+            )
+            copy.start()
+            ring.append(copy)
     got[me] = x_ref[me]
-    settle(got, 0)
     for plane in range(planes):
+        settle(got, 0, plane)
         product = jnp.dot(
             matrix_ref[...],
             got[:, plane].reshape(count * depth, width),
@@ -102,33 +143,45 @@
             preferred_element_type=jnp.float32,
         )
         ready[:, plane] = product.reshape(count, rows, width)
-    second = push(ready, landed, 1)
+        push(ready, landed, 1, plane)
     landed[me] = ready[me]
-    settle(landed, 1)
+    for plane in range(planes):
+        settle(landed, 1, plane)
     if extra_ref is None:
         out_ref[...] = landed[...]
     else:
-        out_ref[...] = landed[...] + extra_ref[...]
-    for copy in first + second:
+        out_ref[...] = landed[...].reshape(out_ref.shape) + extra_ref[...]
+    for copy in started:
         copy.wait_send()
+    for copy in ring:
+        copy.wait()
 
 
 def exchange(matrix, x, extra, which):
     count, planes, depth, width = x.shape
     rows = matrix.shape[0] // count
-    operands = (matrix, x) if extra is None else (matrix, x, extra)
+    around = extra is None
+    operands = (matrix, x) if around else (matrix, x, extra)
+    vmem = pl.BlockSpec(memory_space=pltpu.VMEM)
+    result = jax.ShapeDtypeStruct(
+        (count, planes, rows, width) if around else extra.shape, jnp.float32
+    )
+    ring = jax.ShapeDtypeStruct(x.shape, jnp.float32)
+    scratch = [
+        pltpu.VMEM((count, planes, depth, width), jnp.float32),
+        pltpu.VMEM((count, planes, rows, width), jnp.float32),
+        pltpu.VMEM((count, planes, rows, width), jnp.float32),
+        pltpu.SemaphoreType.DMA((2, planes, count)),
+        pltpu.SemaphoreType.DMA((2, planes, count)),
+    ]
+    if around:
+        scratch += [pltpu.SemaphoreType.DMA((2,)), pltpu.SemaphoreType.DMA((2,))]
     return pl.pallas_call(
-        functools.partial(exchange_body, count),
-        out_shape=jax.ShapeDtypeStruct((count, planes, rows, width), jnp.float32),
-        in_specs=[pl.BlockSpec(memory_space=pltpu.VMEM)] * len(operands),
-        out_specs=pl.BlockSpec(memory_space=pltpu.VMEM),
-        scratch_shapes=[
-            pltpu.VMEM((count, planes, depth, width), jnp.float32),
-            pltpu.VMEM((count, planes, rows, width), jnp.float32),
-            pltpu.VMEM((count, planes, rows, width), jnp.float32),
-            pltpu.SemaphoreType.DMA((2, count)),
-            pltpu.SemaphoreType.DMA((2, count)),
-        ],
+        functools.partial(exchange_body, count, around, lax.axis_size("box")),
+        out_shape=(result, ring, ring) if around else result,
+        in_specs=[vmem] * len(operands),
+        out_specs=(vmem,) * 3 if around else vmem,
+        scratch_shapes=scratch,
         compiler_params=pltpu.CompilerParams(collective_id=which, has_side_effects=True),
         name="exchange_" + str(which),
     )(*operands)
@@ -236,16 +289,18 @@
         theta_interp.reshape(theta_total, dir_count, theta_child),
         ((0, 0), (0, 0), (0, padded - theta_child)),
     ).reshape(theta_total, dir_count * padded)
-    before, after = neighbours(child_rad)
-    theta_done = exchange(
-        spread, jnp.pad(child_rad, grow).reshape(dir_count, planes, padded, phi_child), None, 0
-    )
+    grown = jnp.pad(child_rad, grow)
+    theta_done, before, after = exchange(
+        spread, grown.reshape(dir_count, planes, padded, phi_child), None, 0
+    )
+    before = before.reshape(grown.shape)[:, :, :theta_child]
+    after = after.reshape(grown.shape)[:, :, :theta_child]
     child_trans = translate(
         child_rad, before, after, child_ops, far_child_src, far_child_op, far_child_len, None,
         "child_translate",
     )
     theta_done = theta_done.reshape(child_count, 2, theta_parent, phi_child)
-    interp = jnp.einsum("ncjf,fg->ncjg", theta_done, phi_interp, precision=highest)
+    interp = jnp.einsum("ncjf,fg->ncjg", theta_done, phi_interp, precision=lax.Precision.HIGH)
     cosine, sine = phase_block(
         jnp.arange(8, dtype=jnp.int32), dir_index * theta_parent, theta_parent, theta_total,
         0, phi_parent, phi_parent,
@@ -270,12 +325,12 @@
         ],
         axis=1,
     )
-    back_phi = jnp.einsum("ncjg,fg->ncjf", unshift, phi_interp, precision=highest)
-    extra = jnp.pad(child_trans, grow).reshape(dir_count, planes, padded, phi_child)
+    back_phi = jnp.einsum("ncjg,fg->ncjf", unshift, phi_interp, precision=lax.Precision.HIGH)
+    extra = jnp.pad(child_trans, grow)
     child_local = exchange(
         spread.T, back_phi.reshape(dir_count, planes, theta_parent, phi_child), extra, 1
     )
-    child_local = child_local.reshape(child_count, 2, padded, phi_child)[:, :, :theta_child]
+    child_local = child_local[:, :, :theta_child]
     return (child_local, parent_local, parent_rad)
 
 

time: 138 us -> 124 us (0.90)
  the two profiles are of different devices: /device:TPU:1 before, /device:TPU:0 now
where the time goes in v2:
time: 124 us
  Pallas kernels  91.7 us (74%)
  local copies, waits for them, and re-layouts  13.6 us (11%)
  matrix products  6.22 us (5%)
  other arithmetic  5.78 us (5%)
  starting transfers between devices  5.29 us (4%)
    pallas_call x2, Pallas kernels, exchange(): pl.pallas_call(functools.partial(exchange_body, count, around, lax.axis_s...  84.5 us
    unnamed x42, local copies, waits for them, and re-layouts  8.99 us
    pallas_call x2, Pallas kernels, translate(): pl.pallas_call(functools.partial(translate_body, base is not None), out_s...  7.18 us
    ppermute x2, starting transfers between devices, neighbours(): return (lax.ppermute(array, 'box', up), lax.ppermute(array, 'box', down))  5.29 us
    gather x1, local copies, waits for them, and re-layouts, per_device(): own_field = parent_local[parent_slot]  3.22 us
  transfers between devices with their start and end apart: 2, of which 0 were waited for; matrix products, arithmetic and copies ran while one was open for 1% of the time, Pallas kernels for 3%

profile of v2, /device:TPU:0, one launch (start us, length us, event | category | flops | bytes accessed | tf_op | source)
XLA Modules:
  0.0 123.6 jit_solution(7069357085686627811)
XLA Ops:
  0.7 0.7 compare_select_fusion.1
  1.7 2.0 %fusion.13 = (f32[8,32,512]{2,1,0:T(8,128)S(1)}, f32[8,32,512]{2,1,0:T(8,128)S(1)}) fusion(f32[32,512]{1,0:T(8,128)S(1)} %broadcast_add_fusion, f32[8]{0:T(128)S(1)} %fusion.28, f32[32,512]{1,0:T(8,128)S(1)} %get-tuple-element.25, f32[8]{0:T(128)S(1)} %get-tuple-element.31, f32[32,512]{1,0:T(8,128)S(1)} %get-tuple-element.24, f32[8]{0:T(128)S(1)} %get-tuple-element.30), kind=kLoop, calls=%fused_computation.26 | loop fusion | flops 786432 | bytes 1245280 | tf_op jit(solution)/shard_map/sin | solution.py:44
  3.7 0.6 gather_fusion
  4.3 0.6 gather_fusion.1
  5.0 45.0 %exchange_0.1 = (f32[8,4,32,256]{3,2,1,0:T(8,128)}, f32[8,4,16,256]{3,2,1,0:T(8,128)}, f32[8,4,16,256]{3,2,1,0:T(8,128)}) custom-call(f32[256,128]{1,0:T(8,128)} %matrix_ref.1, f32[8,4,16,256]{3,2,1,0:T(8,128)} %bitcast.45), custom_call_target="tpu_custom_call" | custom-call | tf_op jit(solution)/shard_map/exchange_0/pallas_call | solution.py:179
  50.1 2.2 %fusion.11 = f32[16,2,32,512]{3,2,1,0:T(8,128)S(1)} fusion(f32[16,2,32,256]{3,2,1,0:T(8,128)} %bitcast.49, f32[256,512]{1,0:T(8,128)S(1)} %copy-done), kind=kOutput, calls=%fused_computation.23 | convolution fusion | flops 805306368 | bytes 3670016 | tf_op jit(solution)/shard_map/ncjf,fg->ncjg/dot_general | solution.py:303
  52.3 0.5 fusion.6
  52.8 0.2 pad_maximum_fusion
  53.1 2.0 %fusion.4 = f32[4,2,32,512]{3,0,2,1:T(4,128)S(1)} fusion(f32[16,2,32,512]{3,2,1,0:T(8,128)S(1)} %pad_maximum_fusion, s32[16]{0:T(128)S(1)} %get-tuple-element.17), kind=kOutput, calls=%fused_computation.8 | convolution fusion | flops 25165888 | bytes 2621504 | tf_op jit(solution)/shard_map/pn,ncjg->pcjg/dot_general | solution.py:314
  55.1 0.2 copy.19.refs_4_
  55.3 1.4 %collective-permute-start.1 = (f32[4,2,32,512]{3,2,1,0:T(8,128)S(1)}, f32[4,2,32,512]{3,2,1,0:T(8,128)}, u32[]{:S(2)}, u32[]{:S(2)}) collective-permute-start(f32[4,2,32,512]{3,2,1,0:T(8,128)S(1)} %copy.19.refs_4_), channel_id=1, source_target_pairs={{8,0},{16,8},{24,16},{9,1},{17,9},{25,17},{10,2},{18,10},{26,18},{... | collective-permute-start | bytes 1572872 | tf_op jit(solution)/shard_map/ppermute | solution.py:19
  56.8 3.9 %collective-permute-start = (f32[4,2,32,512]{3,2,1,0:T(8,128)S(1)}, f32[4,2,32,512]{3,2,1,0:T(8,128)}, u32[]{:S(2)}, u32[]{:S(2)}) collective-permute-start(f32[4,2,32,512]{3,2,1,0:T(8,128)S(1)} %copy.19.refs_4_), channel_id=1, source_target_pairs={{0,8},{8,16},{16,24},{1,9},{9,17},{17,25},{2,10},{10,18},{18,26},{... | collective-permute-start | bytes 1572872 | tf_op jit(solution)/shard_map/ppermute | solution.py:19
  60.6 1.7 %copy.17 = f32[256,128]{0,1:T(8,128)} copy(f32[256,128]{1,0:T(8,128)} %matrix_ref.1) | data formatting | bytes 262144 | tf_op args[2]
  62.3 1.0 copy-done.7
  63.4 1.0 copy-done.8
  64.4 3.4 %child_translate.1.refs_0_ = f32[16,2,16,256]{3,2,1,0:T(8,128)S(1)} custom-call(s32[16,16]{1,0:T(8,128)S(1)} %copy-done.9, s32[16,16]{1,0:T(8,128)S(1)} %copy-done.10, s32[16]{0:T(128)S(1)} %copy-done.13, f32[16,2,16,256]{3,2,1,0:T(8,128)S(1)} %bitcast.46, f32[16,2,16,256]{3,2,1,0:T(8,128)S(1)} %copy-done.3, f32[16,2,16,256]{3,2,1,0:T(8,128)S(1)} %bitcast.47, ...), custom_call_target="tpu_custom_call" | custom-call | tf_op jit(solution)/shard_map/child_translate/pallas_call | solution.py:245
  67.8 0.8 copy-done.4
  68.7 2.5 %copy-done.1 = f32[40,2,32,512]{3,2,1,0:T(8,128)S(1)} copy-done((f32[40,2,32,512]{3,2,1,0:T(8,128)S(1)}, f32[40,2,32,512]{3,2,1,0:T(8,128)}, u32[]{:S(2)}) %copy-start.1) | copy-done | bytes 5242904
  71.1 3.8 %parent_translate.1 = f32[4,2,32,512]{3,2,1,0:T(8,128)} custom-call(s32[4,8]{1,0:T(4,128)S(1)} %copy-done.11, s32[4,8]{1,0:T(4,128)S(1)} %copy-done.12, s32[4]{0:T(128)S(1)} %copy-done.14, f32[4,2,32,512]{3,2,1,0:T(8,128)} %collective-permute-done.refs_3_, f32[4,2,32,512]{3,2,1,0:T(8,128)S(1)} %copy.19.refs_4_, ...), custom_call_target="tpu_custom_call" | custom-call | tf_op jit(solution)/shard_map/parent_translate/pallas_call | solution.py:245
  75.0 3.2 %gather_fusion.2 = f32[16,2,32,512]{3,2,1,0:T(8,128)} fusion(f32[4,2,32,512]{3,2,1,0:T(8,128)} %parent_translate.1, s32[1024]{0:T(1024)S(1)} %pad_clamp_fusion), kind=kCustom, calls=%fused_computation.2 | custom fusion | bytes 4194368 | tf_op jit(solution)/shard_map/gather | solution.py:320
  78.2 2.0 %fusion.8 = (f32[16,1,32,512]{3,2,1,0:T(8,128)S(1)}, f32[16,1,32,512]{3,2,1,0:T(8,128)S(1)}) fusion(f32[16,32,512]{2,1,0:T(8,128)S(1)} %copy-done.18, f32[16,32,512]{2,1,0:T(8,128)S(1)} %copy-done.16, f32[16,2,32,512]{3,2,1,0:T(8,128)} %gather_fusion.2), kind=kLoop, calls=%fused_computation.16 | loop fusion | flops 1572864 | bytes 6291456 | tf_op jit(solution)/shard_map/add | solution.py:323
  80.3 2.0 %fusion = f32[16,2,32,256]{3,2,1,0:T(8,128)} fusion(f32[16,1,32,512]{3,2,1,0:T(8,128)S(1)} %get-tuple-element.19, f32[16,1,32,512]{3,2,1,0:T(8,128)S(1)} %get-tuple-element.18, f32[256,512]{1,0:T(8,128)S(1)} %copy-done), kind=kOutput, calls=%fused_computation.4 | convolution fusion | flops 805830656 | bytes 3670016 | tf_op jit(solution)/shard_map/ncjg,fg->ncjf/dot_general | solution.py:328
  82.3 39.4 %exchange_1.1 = f32[16,2,16,256]{3,2,1,0:T(8,128)} custom-call(f32[128,256]{1,0:T(8,128)} %bitcast.50, f32[8,4,32,256]{3,2,1,0:T(8,128)} %bitcast.48, f32[16,2,16,256]{3,2,1,0:T(8,128)} %copy-done.4), custom_call_target="tpu_custom_call" | custom-call | tf_op jit(solution)/shard_map/exchange_1/pallas_call | solution.py:179
  121.7 1.9 %copy.28 = f32[16,2,16,256]{3,2,1,0:T(8,128)} copy(f32[16,2,16,256]{3,2,1,0:T(8,128)} %exchange_1.1) | data formatting | bytes 1048576
  (48 shorter events, 0.4 us)
Async XLA Ops:
  0.6 49.4 %copy-start = (f32[256,512]{1,0:T(8,128)S(1)}, f32[256,512]{1,0:T(8,128)}, u32[]{:S(2)}) copy-start(f32[256,512]{1,0:T(8,128)} %param.17) | copy-start | bytes 1572868
  3.7 1.3 %copy-start.19 = (s32[16]{0:T(128)S(1)}, s32[16]{0:T(128)}, u32[]{:S(2)}) copy-start(s32[16]{0:T(128)} %param.20) | copy-start | bytes 196
  4.3 48.0 %copy-start.15 = (f32[16,32,512]{2,1,0:T(8,128)}, f32[16,32,512]{2,1,0:T(8,128)S(1)}, u32[]{:S(2)}) copy-start(f32[16,32,512]{2,1,0:T(8,128)S(1)} %gather_fusion) | copy-start | bytes 3145732
  5.0 47.4 %copy-start.17 = (f32[16,32,512]{2,1,0:T(8,128)}, f32[16,32,512]{2,1,0:T(8,128)S(1)}, u32[]{:S(2)}) copy-start(f32[16,32,512]{2,1,0:T(8,128)S(1)} %gather_fusion.1) | copy-start | bytes 3145732
  53.1 9.2 %copy-start.3 = (f32[16,2,16,256]{3,2,1,0:T(8,128)S(1)}, f32[16,2,16,256]{3,2,1,0:T(8,128)}, u32[]{:S(2)}) copy-start(f32[16,2,16,256]{3,2,1,0:T(8,128)} %refs_4_.1) | copy-start | bytes 1572868
  53.1 9.2 %copy-start.5 = (f32[40,2,16,256]{3,2,1,0:T(8,128)S(1)}, f32[40,2,16,256]{3,2,1,0:T(8,128)}, u32[]{:S(2)}) copy-start(f32[40,2,16,256]{3,2,1,0:T(8,128)} %refs_6_.3) | copy-start | bytes 3932164
  53.1 9.2 %copy-start.9 = (s32[16,16]{1,0:T(8,128)S(1)}, s32[16,16]{1,0:T(8,128)}, u32[]{:S(2)}) copy-start(s32[16,16]{1,0:T(8,128)} %refs_0_.3) | copy-start | bytes 3076
  53.1 9.2 %copy-start.10 = (s32[16,16]{1,0:T(8,128)S(1)}, s32[16,16]{1,0:T(8,128)}, u32[]{:S(2)}) copy-start(s32[16,16]{1,0:T(8,128)} %refs_1_.3) | copy-start | bytes 3076
  53.1 9.2 %copy-start.13 = (s32[16]{0:T(128)S(1)}, s32[16]{0:T(128)}, u32[]{:S(2)}) copy-start(s32[16]{0:T(128)} %refs_2_.3) | copy-start | bytes 196
  55.1 13.5 %copy-start.11 = (s32[4,8]{1,0:T(4,128)S(1)}, s32[4,8]{1,0:T(4,128)}, u32[]{:S(2)}) copy-start(s32[4,8]{1,0:T(4,128)} %refs_0_.2) | copy-start | bytes 388
  55.1 13.5 %copy-start.12 = (s32[4,8]{1,0:T(4,128)S(1)}, s32[4,8]{1,0:T(4,128)}, u32[]{:S(2)}) copy-start(s32[4,8]{1,0:T(4,128)} %refs_1_.2) | copy-start | bytes 388
  55.1 13.5 %copy-start.14 = (s32[4]{0:T(128)S(1)}, s32[4]{0:T(128)}, u32[]{:S(2)}) copy-start(s32[4]{0:T(128)} %refs_2_.2) | copy-start | bytes 52
  55.3 19.7 %copy-start.2 = (f32[4,2,32,512]{3,2,1,0:T(8,128)}, f32[4,2,32,512]{3,2,1,0:T(8,128)S(1)}, u32[]{:S(2)}) copy-start(f32[4,2,32,512]{3,2,1,0:T(8,128)S(1)} %copy.19.refs_4_) | copy-start | bytes 1572868
  55.3 13.3 %copy-start.6 = (f32[4,2,32,512]{3,2,1,0:T(8,128)S(1)}, f32[4,2,32,512]{3,2,1,0:T(8,128)}, u32[]{:S(2)}) copy-start(f32[4,2,32,512]{3,2,1,0:T(8,128)} %refs_7_.1) | copy-start | bytes 1572868
  55.3 13.3 %collective-permute-start.1 = (f32[4,2,32,512]{3,2,1,0:T(8,128)S(1)}, f32[4,2,32,512]{3,2,1,0:T(8,128)}, u32[]{:S(2)}, u32[]{:S(2)}) collective-permute-start(f32[4,2,32,512]{3,2,1,0:T(8,128)S(1)} %copy.19.refs_4_), channel_id=1, source_target_pairs={{8,0},{16,8},{24,16},{9,1},{17,9},{25,17},{10,2},{18,10},{26,18},{... | collective-permute-start | bytes 1572872 | tf_op jit(solution)/shard_map/ppermute | solution.py:19
  56.8 11.8 %collective-permute-start = (f32[4,2,32,512]{3,2,1,0:T(8,128)S(1)}, f32[4,2,32,512]{3,2,1,0:T(8,128)}, u32[]{:S(2)}, u32[]{:S(2)}) collective-permute-start(f32[4,2,32,512]{3,2,1,0:T(8,128)S(1)} %copy.19.refs_4_), channel_id=1, source_target_pairs={{0,8},{8,16},{16,24},{1,9},{9,17},{17,25},{2,10},{10,18},{18,26},{... | collective-permute-start | bytes 1572872 | tf_op jit(solution)/shard_map/ppermute | solution.py:19
  62.3 1.0 copy-start.7
  63.4 1.0 copy-start.8
  67.8 0.8 copy-start.4
  68.6 2.5 %copy-start.1 = (f32[40,2,32,512]{3,2,1,0:T(8,128)S(1)}, f32[40,2,32,512]{3,2,1,0:T(8,128)}, u32[]{:S(2)}) copy-start(f32[40,2,32,512]{3,2,1,0:T(8,128)} %refs_6_.2) | copy-start | bytes 15728644
  75.0 3.2 %copy-start.16 = (f32[16,32,512]{2,1,0:T(8,128)S(1)}, f32[16,32,512]{2,1,0:T(8,128)}, u32[]{:S(2)}) copy-start(f32[16,32,512]{2,1,0:T(8,128)} %copy-done.15) | copy-start | bytes 3145732
  75.0 3.2 %copy-start.18 = (f32[16,32,512]{2,1,0:T(8,128)S(1)}, f32[16,32,512]{2,1,0:T(8,128)}, u32[]{:S(2)}) copy-start(f32[16,32,512]{2,1,0:T(8,128)} %copy-done.17) | copy-start | bytes 3145732

commit v3 on v2

--- a/solution.py
+++ b/solution.py
@@ -56,7 +56,6 @@
 
 def exchange_body(count, around, fields, matrix_ref, x_ref, *refs):
     refs = list(refs)
-    extra_ref = None if around else refs.pop(0)
     out_ref = refs.pop(0)
     if around:
         below_ref, above_ref = refs.pop(0), refs.pop(0)
@@ -119,6 +118,18 @@
     started = []
     for plane in range(planes):
         push(x_ref, got, 0, plane)
+    got[me] = x_ref[me]
+    for plane in range(planes):
+        settle(got, 0, plane)
+        product = lax.dot_general(
+            matrix_ref[...],
+            got[:, plane].reshape(count * depth, width),
+            (((1 if around else 0,), (0,)), ((), ())),
+            precision=highest,
+            preferred_element_type=jnp.float32,
+        )
+        ready[:, plane] = product.reshape(count, rows, width)
+        push(ready, landed, 1, plane)
     ring = []
     if around:
         box_send, box_recv = refs[5:7]
@@ -133,39 +144,22 @@
             )
             copy.start()
             ring.append(copy)
-    got[me] = x_ref[me]
-    for plane in range(planes):
-        settle(got, 0, plane)
-        product = jnp.dot(
-            matrix_ref[...],
-            got[:, plane].reshape(count * depth, width),
-            precision=highest,
-            preferred_element_type=jnp.float32,
-        )
-        ready[:, plane] = product.reshape(count, rows, width)
-        push(ready, landed, 1, plane)
     landed[me] = ready[me]
     for plane in range(planes):
         settle(landed, 1, plane)
-    if extra_ref is None:
-        out_ref[...] = landed[...]
-    else:
-        out_ref[...] = landed[...].reshape(out_ref.shape) + extra_ref[...]
+    out_ref[...] = landed[...].reshape(out_ref.shape)
     for copy in started:
         copy.wait_send()
     for copy in ring:
         copy.wait()
 
 
-def exchange(matrix, x, extra, which):
+def exchange(matrix, x, around, which):
     count, planes, depth, width = x.shape
-    rows = matrix.shape[0] // count
-    around = extra is None
-    operands = (matrix, x) if around else (matrix, x, extra)
+    rows = matrix.shape[0 if around else 1] // count
+    operands = (matrix, x)
     vmem = pl.BlockSpec(memory_space=pltpu.VMEM)
-    result = jax.ShapeDtypeStruct(
-        (count, planes, rows, width) if around else extra.shape, jnp.float32
-    )
+    result = jax.ShapeDtypeStruct((count * planes, rows, width), jnp.float32)
     ring = jax.ShapeDtypeStruct(x.shape, jnp.float32)
     scratch = [
         pltpu.VMEM((count, planes, depth, width), jnp.float32),
@@ -182,7 +176,9 @@
         in_specs=[vmem] * len(operands),
         out_specs=(vmem,) * 3 if around else vmem,
         scratch_shapes=scratch,
-        compiler_params=pltpu.CompilerParams(collective_id=which, has_side_effects=True),
+        compiler_params=pltpu.CompilerParams(
+            collective_id=which, has_side_effects=True, vmem_limit_bytes=16 * 1024 * 1024
+        ),
         name="exchange_" + str(which),
     )(*operands)
 
@@ -236,7 +232,7 @@
     boxes = own.shape[0]
     vmem = pl.BlockSpec(memory_space=pltpu.VMEM)
     smem = pl.BlockSpec(memory_space=pltpu.SMEM)
-    anywhere = pl.BlockSpec(memory_space=pl.ANY)
+    anywhere = pl.BlockSpec(memory_space=pltpu.HBM)
     operands = [source, which_op, length, before, own, after, operators]
     specs = [smem] * 3 + [anywhere] * 3 + [vmem]
     if base is not None:
@@ -251,9 +247,53 @@
             pltpu.VMEM((3 * boxes,) + own.shape[1:], jnp.float32),
             pltpu.SemaphoreType.DMA((3,)),
         ],
-        compiler_params=pltpu.CompilerParams(vmem_limit_bytes=40 * 1024 * 1024),
+        compiler_params=pltpu.CompilerParams(vmem_limit_bytes=20 * 1024 * 1024),
         name=name,
     )(*operands)
+
+
+def shift_body(parent_ref, octant_ref, cosine_ref, sine_ref, interp_ref, out_ref):
+    children = interp_ref.shape[0]
+    offset = lax.axis_index("box") * out_ref.shape[0]
+    out_ref[...] = jnp.zeros_like(out_ref)
+
+    def one_child(child, carry):
+        slot, octant = parent_ref[child] - offset, octant_ref[child]
+        cosine, sine = cosine_ref[octant], sine_ref[octant]
+        real, imag = interp_ref[child, 0], interp_ref[child, 1]
+        out_ref[slot, 0] += cosine * real - sine * imag
+        out_ref[slot, 1] += sine * real + cosine * imag
+        return carry
+
+    lax.fori_loop(0, children, one_child, 0)
+
+
+def unshift_body(parent_ref, octant_ref, cosine_ref, sine_ref, field_ref, out_ref):
+    children = out_ref.shape[0]
+    offset = lax.axis_index("box") * field_ref.shape[0]
+
+    def one_child(child, carry):
+        slot, octant = parent_ref[child] - offset, octant_ref[child]
+        cosine, sine = cosine_ref[octant], sine_ref[octant]
+        real, imag = field_ref[slot, 0], field_ref[slot, 1]
+        out_ref[child, 0] = cosine * real + sine * imag
+        out_ref[child, 1] = cosine * imag - sine * real
+        return carry
+
+    lax.fori_loop(0, children, one_child, 0)
+
+
+def by_child(body, parent, octant, cosine, sine, values, boxes, name):
+    vmem = pl.BlockSpec(memory_space=pltpu.VMEM)
+    smem = pl.BlockSpec(memory_space=pltpu.SMEM)
+    return pl.pallas_call(
+        body,
+        out_shape=jax.ShapeDtypeStruct((boxes,) + values.shape[1:], jnp.float32),
+        in_specs=[smem] * 2 + [vmem] * 3,
+        out_specs=vmem,
+        compiler_params=pltpu.CompilerParams(vmem_limit_bytes=16 * 1024 * 1024),
+        name=name,
+    )(parent, octant, cosine, sine, values)
 
 
 def per_device(
@@ -278,12 +318,7 @@
     dir_count = lax.axis_size("dir")
     planes = child_count * 2 // dir_count
     padded = -(-theta_child // 8) * 8
-    box_index = lax.axis_index("box")
     dir_index = lax.axis_index("dir")
-    parent_slot = child_parent - box_index * parent_count
-    member = (parent_slot[None, :] == jnp.arange(parent_count, dtype=jnp.int32)[:, None]).astype(
-        jnp.float32
-    )
     grow = ((0, 0), (0, 0), (0, padded - theta_child), (0, 0))
     spread = jnp.pad(
         theta_interp.reshape(theta_total, dir_count, theta_child),
@@ -291,7 +326,7 @@
     ).reshape(theta_total, dir_count * padded)
     grown = jnp.pad(child_rad, grow)
     theta_done, before, after = exchange(
-        spread, grown.reshape(dir_count, planes, padded, phi_child), None, 0
+        spread, grown.reshape(dir_count, planes, padded, phi_child), True, 0
     )
     before = before.reshape(grown.shape)[:, :, :theta_child]
     after = after.reshape(grown.shape)[:, :, :theta_child]
@@ -305,32 +340,23 @@
         jnp.arange(8, dtype=jnp.int32), dir_index * theta_parent, theta_parent, theta_total,
         0, phi_parent, phi_parent,
     )
-    cosine, sine = lax.optimization_barrier((cosine, sine))
-    cosine, sine = cosine[child_octant], sine[child_octant]
-    shifted = jnp.stack(
-        [cosine * interp[:, 0] - sine * interp[:, 1], sine * interp[:, 0] + cosine * interp[:, 1]],
-        axis=1,
-    )
-    parent_rad = jnp.einsum("pn,ncjg->pcjg", member, shifted, precision=highest)
+    parent_rad = by_child(
+        shift_body, child_parent, child_octant, cosine, sine, interp, parent_count, "shift"
+    )
     before, after = neighbours(parent_rad)
     parent_local = translate(
         parent_rad, before, after, parent_ops, far_parent_src, far_parent_op, far_parent_len,
         parent_incoming, "parent_translate",
     )
-    own_field = parent_local[parent_slot]
-    unshift = jnp.stack(
-        [
-            cosine * own_field[:, 0] + sine * own_field[:, 1],
-            cosine * own_field[:, 1] - sine * own_field[:, 0],
-        ],
-        axis=1,
+    unshift = by_child(
+        unshift_body, child_parent, child_octant, cosine, sine, parent_local, child_count, "unshift"
     )
     back_phi = jnp.einsum("ncjg,fg->ncjf", unshift, phi_interp, precision=lax.Precision.HIGH)
-    extra = jnp.pad(child_trans, grow)
-    child_local = exchange(
-        spread.T, back_phi.reshape(dir_count, planes, theta_parent, phi_child), extra, 1
-    )
-    child_local = child_local[:, :, :theta_child]
+    anterp = exchange(
+        spread, back_phi.reshape(dir_count, planes, theta_parent, phi_child), False, 1
+    )
+    anterp = anterp.reshape(child_count, 2, padded, phi_child)[:, :, :theta_child]
+    child_local = child_trans + anterp
     return (child_local, parent_local, parent_rad)
 
 

time: 124 us -> 102 us (0.82)
  the two profiles are of different devices: /device:TPU:0 before, /device:TPU:1 now
where the time goes in v3:
time: 102 us
  Pallas kernels  81.8 us (80%)
  starting transfers between devices  6.46 us (6%)
  waiting for transfers between devices  4.57 us (4%)
  other arithmetic  3.16 us (3%)
  local copies, waits for them, and re-layouts  3.08 us (3%)
  matrix products  2.01 us (2%)
    pallas_call x2, Pallas kernels, exchange(): pl.pallas_call(functools.partial(exchange_body, count, around, lax.axis_s...  74.7 us
    ppermute x2, starting transfers between devices, neighbours(): return (lax.ppermute(array, 'box', up), lax.ppermute(array, 'box', down))  6.46 us
    ppermute x2, waiting for transfers between devices, neighbours(): return (lax.ppermute(array, 'box', up), lax.ppermute(array, 'box', down))  4.57 us
    pallas_call x2, Pallas kernels, translate(): pl.pallas_call(functools.partial(translate_body, base is not None), out_s...  4.48 us
    unnamed x36, local copies, waits for them, and re-layouts  3.08 us
    pallas_call x2, Pallas kernels, by_child(): pl.pallas_call(body, out_shape=jax.ShapeDtypeStruct((boxes,) + values.sha...  2.69 us
  transfers between devices with their start and end apart: 2, of which 2 were waited for; matrix products, arithmetic and copies ran while one was open for 0% of the time, Pallas kernels for 2%

profile of v3, /device:TPU:1, one launch (start us, length us, event | category | flops | bytes accessed | tf_op | source)
XLA Modules:
  0.0 102.1 jit_solution(3042067955438845433)
XLA Ops:
  0.6 0.0 copy-start
  0.8 0.1 broadcast_add_fusion
  0.9 1.0 %copy-done.2 = f32[16,2,16,256]{3,2,1,0:T(8,128)S(1)} copy-done((f32[16,2,16,256]{3,2,1,0:T(8,128)S(1)}, f32[16,2,16,256]{3,2,1,0:T(8,128)}, u32[]{:S(2)}) %copy-start.2) | copy-done | bytes 524312
  1.9 0.9 copy-done.8
  2.8 40.7 %exchange_0.1 = (f32[32,32,256]{2,1,0:T(8,128)S(1)}, f32[8,4,16,256]{3,2,1,0:T(8,128)S(1)}, f32[8,4,16,256]{3,2,1,0:T(8,128)S(1)}) custom-call(f32[256,128]{1,0:T(8,128)S(1)} %copy-done.8, f32[8,4,16,256]{3,2,1,0:T(8,128)S(1)} %bitcast.17), custom_call_target="tpu_custom_call" | custom-call | tf_op jit(solution)/shard_map/exchange_0/pallas_call | solution.py:173
  43.5 0.0 copy-start.14
  43.5 1.0 fusion.2.interp_ref
  44.5 0.1 broadcast_multiply_fusion.1
  44.6 2.0 %fusion.4 = (f32[8,32,512]{2,1,0:T(8,128)S(1)}, f32[8,32,512]{2,1,0:T(8,128)S(1)}) fusion(f32[32,512]{1,0:T(8,128)S(1)} %broadcast_add_fusion, f32[8]{0:T(128)S(1)} %fusion.16, f32[32,512]{1,0:T(8,128)S(1)} %get-tuple-element.12, f32[8]{0:T(128)S(1)} %get-tuple-element.18, f32[32,512]{1,0:T(8,128)S(1)} %get-tuple-element.11, f32[8]{0:T(128)S(1)} %get-tuple-element.17), kind=kLoop, calls=%fused_computation.5 | loop fusion | flops 786432 | bytes 1245280 | tf_op jit(solution)/shard_map/sin | solution.py:44
  46.7 0.0 copy-start.11
  46.7 0.0 copy-start.16
  46.7 1.8 %shift.1.refs_4_ = f32[4,2,32,512]{3,2,1,0:T(8,128)} custom-call(s32[16]{0:T(128)S(1)} %copy-done.14, s32[16]{0:T(128)S(1)} %copy-done.15, f32[8,32,512]{2,1,0:T(8,128)S(1)} %get-tuple-element.10.cosine_ref, f32[8,32,512]{2,1,0:T(8,128)S(1)} %get-tuple-element.9.sine_ref, f32[16,2,32,512]{3,2,1,0:T(8,128)S(1)} %fusion.2.interp_ref), custom_call_target="tpu_custom_call" | custom-call | tf_op jit(solution)/shard_map/shift/pallas_call | solution.py:289
  48.5 3.7 %collective-permute-start.1 = (f32[4,2,32,512]{3,2,1,0:T(8,128)}, f32[4,2,32,512]{3,2,1,0:T(8,128)S(1)}, u32[]{:S(2)}, u32[]{:S(2)}) collective-permute-start(f32[4,2,32,512]{3,2,1,0:T(8,128)} %shift.1.refs_4_), channel_id=1, source_target_pairs={{8,0},{16,8},{24,16},{9,1},{17,9},{25,17},{10,2},{18,10},{26,18},{... | collective-permute-start | bytes 1572872 | tf_op jit(solution)/shard_map/ppermute | solution.py:19
  52.2 2.8 %collective-permute-start = (f32[4,2,32,512]{3,2,1,0:T(8,128)}, f32[4,2,32,512]{3,2,1,0:T(8,128)S(1)}, u32[]{:S(2)}, u32[]{:S(2)}) collective-permute-start(f32[4,2,32,512]{3,2,1,0:T(8,128)} %shift.1.refs_4_), channel_id=1, source_target_pairs={{0,8},{8,16},{16,24},{1,9},{9,17},{17,25},{2,10},{10,18},{18,26},{... | collective-permute-start | bytes 1572872 | tf_op jit(solution)/shard_map/ppermute | solution.py:19
  55.1 1.8 %child_translate.1 = f32[16,2,16,256]{3,2,1,0:T(8,128)S(1)} custom-call(s32[16,16]{1,0:T(8,128)S(1)} %copy-done.10, s32[16,16]{1,0:T(8,128)S(1)} %copy-done.11, s32[16]{0:T(128)S(1)} %copy-done.16, f32[16,2,16,256]{3,2,1,0:T(8,128)S(1)} %bitcast.19, f32[16,2,16,256]{3,2,1,0:T(8,128)S(1)} %copy-done.3, f32[16,2,16,256]{3,2,1,0:T(8,128)S(1)} %bitcast.20, ...), custom_call_target="tpu_custom_call" | custom-call | tf_op jit(solution)/shard_map/child_translate/pallas_call | solution.py:241
  56.9 3.3 %collective-permute-done.1.refs_5_ = f32[4,2,32,512]{3,2,1,0:T(8,128)S(1)} collective-permute-done((f32[4,2,32,512]{3,2,1,0:T(8,128)}, f32[4,2,32,512]{3,2,1,0:T(8,128)S(1)}, u32[]{:S(2)}, u32[]{:S(2)}) %collective-permute-start.1) | collective-permute-done | bytes 524320 | tf_op jit(solution)/shard_map/ppermute | solution.py:19
  60.1 1.3 %collective-permute-done.refs_3_ = f32[4,2,32,512]{3,2,1,0:T(8,128)S(1)} collective-permute-done((f32[4,2,32,512]{3,2,1,0:T(8,128)}, f32[4,2,32,512]{3,2,1,0:T(8,128)S(1)}, u32[]{:S(2)}, u32[]{:S(2)}) %collective-permute-start) | collective-permute-done | bytes 524320 | tf_op jit(solution)/shard_map/ppermute | solution.py:19
  61.5 2.7 %parent_translate.1.field_ref = f32[4,2,32,512]{3,2,1,0:T(8,128)} custom-call(s32[4,8]{1,0:T(4,128)S(1)} %copy-done.12, s32[4,8]{1,0:T(4,128)S(1)} %copy-done.13, s32[4]{0:T(128)S(1)} %copy-done.17, f32[4,2,32,512]{3,2,1,0:T(8,128)S(1)} %collective-permute-done.refs_3_, f32[4,2,32,512]{3,2,1,0:T(8,128)S(1)} %copy-done.4, ...), custom_call_target="tpu_custom_call" | custom-call | tf_op jit(solution)/shard_map/parent_translate/pallas_call | solution.py:241
  64.2 0.0 copy-start.5
  64.2 1.0 %copy-done.5 = f32[4,2,32,512]{3,2,1,0:T(8,128)S(1)} copy-done((f32[4,2,32,512]{3,2,1,0:T(8,128)S(1)}, f32[4,2,32,512]{3,2,1,0:T(8,128)}, u32[]{:S(2)}) %copy-start.5) | copy-done | bytes 524312
  65.2 0.9 unshift.1
  66.1 1.0 %fusion = f32[16,2,32,256]{3,2,1,0:T(8,128)S(1)} fusion(f32[16,2,32,512]{3,2,1,0:T(8,128)S(1)} %unshift.1, f32[256,512]{1,0:T(8,128)S(1)} %copy-done), kind=kOutput, calls=%fused_computation | convolution fusion | flops 805306368 | bytes 3670016 | tf_op jit(solution)/shard_map/ncjg,fg->ncjf/dot_general | solution.py:354
  67.2 34.0 %exchange_1.1 = f32[32,16,256]{2,1,0:T(8,128)S(1)} custom-call(f32[256,128]{1,0:T(8,128)S(1)} %copy-done.9, f32[8,4,32,256]{3,2,1,0:T(8,128)S(1)} %bitcast.15), custom_call_target="tpu_custom_call" | custom-call | tf_op jit(solution)/shard_map/exchange_1/pallas_call | solution.py:173
  101.2 0.9 add.100
  (33 shorter events, 0.2 us)
Async XLA Ops:
  0.6 42.9 %copy-start = (f32[256,512]{1,0:T(8,128)S(1)}, f32[256,512]{1,0:T(8,128)}, u32[]{:S(2)}) copy-start(f32[256,512]{1,0:T(8,128)} %param.17) | copy-start | bytes 1572868
  0.9 1.0 %copy-start.2 = (f32[16,2,16,256]{3,2,1,0:T(8,128)S(1)}, f32[16,2,16,256]{3,2,1,0:T(8,128)}, u32[]{:S(2)}) copy-start(f32[16,2,16,256]{3,2,1,0:T(8,128)} %refs_4_.1) | copy-start | bytes 1572868
  1.9 0.9 copy-start.8
  43.5 3.2 %copy-start.14 = (s32[16]{0:T(128)S(1)}, s32[16]{0:T(128)}, u32[]{:S(2)}) copy-start(s32[16]{0:T(128)} %parent_ref.3) | copy-start | bytes 196
  43.5 3.2 %copy-start.15 = (s32[16]{0:T(128)S(1)}, s32[16]{0:T(128)}, u32[]{:S(2)}) copy-start(s32[16]{0:T(128)} %octant_ref.3) | copy-start | bytes 196
  44.6 10.4 %copy-start.6 = (f32[40,2,16,256]{3,2,1,0:T(8,128)S(1)}, f32[40,2,16,256]{3,2,1,0:T(8,128)}, u32[]{:S(2)}) copy-start(f32[40,2,16,256]{3,2,1,0:T(8,128)} %refs_6_.2) | copy-start | bytes 3932164
  46.6 8.4 %copy-start.3 = (f32[16,2,16,256]{3,2,1,0:T(8,128)S(1)}, f32[16,2,16,256]{3,2,1,0:T(8,128)}, u32[]{:S(2)}) copy-start(f32[16,2,16,256]{3,2,1,0:T(8,128)} %refs_4_.1) | copy-start | bytes 1572868
  46.6 8.4 %copy-start.10 = (s32[16,16]{1,0:T(8,128)S(1)}, s32[16,16]{1,0:T(8,128)}, u32[]{:S(2)}) copy-start(s32[16,16]{1,0:T(8,128)} %refs_0_.2) | copy-start | bytes 3076
  46.7 8.4 %copy-start.11 = (s32[16,16]{1,0:T(8,128)S(1)}, s32[16,16]{1,0:T(8,128)}, u32[]{:S(2)}) copy-start(s32[16,16]{1,0:T(8,128)} %refs_1_.2) | copy-start | bytes 3076
  46.7 8.4 %copy-start.16 = (s32[16]{0:T(128)S(1)}, s32[16]{0:T(128)}, u32[]{:S(2)}) copy-start(s32[16]{0:T(128)} %refs_2_.2) | copy-start | bytes 196
  46.7 14.7 %copy-start.1 = (f32[40,2,32,512]{3,2,1,0:T(8,128)S(1)}, f32[40,2,32,512]{3,2,1,0:T(8,128)}, u32[]{:S(2)}) copy-start(f32[40,2,32,512]{3,2,1,0:T(8,128)} %refs_6_.3) | copy-start | bytes 15728644
  48.5 12.9 %copy-start.4 = (f32[4,2,32,512]{3,2,1,0:T(8,128)S(1)}, f32[4,2,32,512]{3,2,1,0:T(8,128)}, u32[]{:S(2)}) copy-start(f32[4,2,32,512]{3,2,1,0:T(8,128)} %shift.1.refs_4_) | copy-start | bytes 1572868
  48.5 12.9 %copy-start.7 = (f32[4,2,32,512]{3,2,1,0:T(8,128)S(1)}, f32[4,2,32,512]{3,2,1,0:T(8,128)}, u32[]{:S(2)}) copy-start(f32[4,2,32,512]{3,2,1,0:T(8,128)} %refs_7_.1) | copy-start | bytes 1572868
  48.5 12.9 %copy-start.12 = (s32[4,8]{1,0:T(4,128)S(1)}, s32[4,8]{1,0:T(4,128)}, u32[]{:S(2)}) copy-start(s32[4,8]{1,0:T(4,128)} %refs_0_.3) | copy-start | bytes 388
  48.5 12.9 %copy-start.13 = (s32[4,8]{1,0:T(4,128)S(1)}, s32[4,8]{1,0:T(4,128)}, u32[]{:S(2)}) copy-start(s32[4,8]{1,0:T(4,128)} %refs_1_.3) | copy-start | bytes 388
  48.5 12.9 %copy-start.17 = (s32[4]{0:T(128)S(1)}, s32[4]{0:T(128)}, u32[]{:S(2)}) copy-start(s32[4]{0:T(128)} %refs_2_.3) | copy-start | bytes 52
  48.5 11.6 %collective-permute-start.1 = (f32[4,2,32,512]{3,2,1,0:T(8,128)}, f32[4,2,32,512]{3,2,1,0:T(8,128)S(1)}, u32[]{:S(2)}, u32[]{:S(2)}) collective-permute-start(f32[4,2,32,512]{3,2,1,0:T(8,128)} %shift.1.refs_4_), channel_id=1, source_target_pairs={{8,0},{16,8},{24,16},{9,1},{17,9},{25,17},{10,2},{18,10},{26,18},{... | collective-permute-start | bytes 1572872 | tf_op jit(solution)/shard_map/ppermute | solution.py:19
  52.2 9.2 %collective-permute-start = (f32[4,2,32,512]{3,2,1,0:T(8,128)}, f32[4,2,32,512]{3,2,1,0:T(8,128)S(1)}, u32[]{:S(2)}, u32[]{:S(2)}) collective-permute-start(f32[4,2,32,512]{3,2,1,0:T(8,128)} %shift.1.refs_4_), channel_id=1, source_target_pairs={{0,8},{8,16},{16,24},{1,9},{9,17},{17,25},{2,10},{10,18},{18,26},{... | collective-permute-start | bytes 1572872 | tf_op jit(solution)/shard_map/ppermute | solution.py:19
  64.2 1.0 %copy-start.5 = (f32[4,2,32,512]{3,2,1,0:T(8,128)S(1)}, f32[4,2,32,512]{3,2,1,0:T(8,128)}, u32[]{:S(2)}) copy-start(f32[4,2,32,512]{3,2,1,0:T(8,128)} %parent_translate.1.field_ref) | copy-start | bytes 1572868
  66.1 1.0 %copy-start.9 = (f32[256,128]{1,0:T(8,128)S(1)}, f32[256,128]{1,0:T(8,128)}, u32[]{:S(2)}) copy-start(f32[256,128]{1,0:T(8,128)} %matrix_ref.3) | copy-start | bytes 393220

commit v4 on v3

--- a/solution.py
+++ b/solution.py
@@ -125,7 +125,7 @@
             matrix_ref[...],
             got[:, plane].reshape(count * depth, width),
             (((1 if around else 0,), (0,)), ((), ())),
-            precision=highest,
+            precision=lax.Precision.HIGH,
             preferred_element_type=jnp.float32,
         )
         ready[:, plane] = product.reshape(count, rows, width)
@@ -259,7 +259,10 @@
 
     def one_child(child, carry):
         slot, octant = parent_ref[child] - offset, octant_ref[child]
-        cosine, sine = cosine_ref[octant], sine_ref[octant]
+        mirrored = octant // 4
+        held = octant + mirrored * (7 - 2 * octant)
+        sign = (1 - 2 * mirrored).astype(jnp.float32)
+        cosine, sine = cosine_ref[held], sign * sine_ref[held]
         real, imag = interp_ref[child, 0], interp_ref[child, 1]
         out_ref[slot, 0] += cosine * real - sine * imag
         out_ref[slot, 1] += sine * real + cosine * imag
@@ -274,7 +277,10 @@
 
     def one_child(child, carry):
         slot, octant = parent_ref[child] - offset, octant_ref[child]
-        cosine, sine = cosine_ref[octant], sine_ref[octant]
+        mirrored = octant // 4
+        held = octant + mirrored * (7 - 2 * octant)
+        sign = (1 - 2 * mirrored).astype(jnp.float32)
+        cosine, sine = cosine_ref[held], sign * sine_ref[held]
         real, imag = field_ref[slot, 0], field_ref[slot, 1]
         out_ref[child, 0] = cosine * real + sine * imag
         out_ref[child, 1] = cosine * imag - sine * real
@@ -337,7 +343,7 @@
     theta_done = theta_done.reshape(child_count, 2, theta_parent, phi_child)
     interp = jnp.einsum("ncjf,fg->ncjg", theta_done, phi_interp, precision=lax.Precision.HIGH)
     cosine, sine = phase_block(
-        jnp.arange(8, dtype=jnp.int32), dir_index * theta_parent, theta_parent, theta_total,
+        jnp.arange(4, dtype=jnp.int32), dir_index * theta_parent, theta_parent, theta_total,
         0, phi_parent, phi_parent,
     )
     parent_rad = by_child(

time: 102 us -> 102 us (level)
  no operation moved by 1% of the time
where the time goes in v4:
time: 102 us
  Pallas kernels  82.5 us (81%)
  starting transfers between devices  6.46 us (6%)
  waiting for transfers between devices  4.55 us (4%)
  local copies, waits for them, and re-layouts  3.08 us (3%)
  other arithmetic  2.18 us (2%)
  matrix products  2.01 us (2%)
    pallas_call x2, Pallas kernels, exchange(): pl.pallas_call(functools.partial(exchange_body, count, around, lax.axis_s...  75.2 us
    ppermute x2, starting transfers between devices, neighbours(): return (lax.ppermute(array, 'box', up), lax.ppermute(array, 'box', down))  6.46 us
    ppermute x2, waiting for transfers between devices, neighbours(): return (lax.ppermute(array, 'box', up), lax.ppermute(array, 'box', down))  4.55 us
    pallas_call x2, Pallas kernels, translate(): pl.pallas_call(functools.partial(translate_body, base is not None), out_s...  4.22 us
    unnamed x36, local copies, waits for them, and re-layouts  3.08 us
    pallas_call x2, Pallas kernels, by_child(): pl.pallas_call(body, out_shape=jax.ShapeDtypeStruct((boxes,) + values.sha...  3 us
  transfers between devices with their start and end apart: 2, of which 2 were waited for; matrix products, arithmetic and copies ran while one was open for 0% of the time, Pallas kernels for 2%

profile of v4, /device:TPU:1, one launch (start us, length us, event | category | flops | bytes accessed | tf_op | source)
XLA Modules:
  0.0 101.7 jit_solution(920456241072307555)
XLA Ops:
  0.6 0.0 copy-start
  0.8 0.1 broadcast_add_fusion
  0.9 1.0 %copy-done.2 = f32[16,2,16,256]{3,2,1,0:T(8,128)S(1)} copy-done((f32[16,2,16,256]{3,2,1,0:T(8,128)S(1)}, f32[16,2,16,256]{3,2,1,0:T(8,128)}, u32[]{:S(2)}) %copy-start.2) | copy-done | bytes 524312
  1.9 0.9 copy-done.8
  2.8 40.7 %exchange_0.1 = (f32[32,32,256]{2,1,0:T(8,128)S(1)}, f32[8,4,16,256]{3,2,1,0:T(8,128)S(1)}, f32[8,4,16,256]{3,2,1,0:T(8,128)S(1)}) custom-call(f32[256,128]{1,0:T(8,128)S(1)} %copy-done.8, f32[8,4,16,256]{3,2,1,0:T(8,128)S(1)} %bitcast.17), custom_call_target="tpu_custom_call" | custom-call | tf_op jit(solution)/shard_map/exchange_0/pallas_call | solution.py:173
  43.5 0.0 copy-start.15
  43.5 0.0 copy-start.6
  43.5 1.0 fusion.2.interp_ref
  44.5 0.0 copy-start.10
  44.6 0.1 broadcast_multiply_fusion.1
  44.7 1.0 %fusion.4 = (f32[4,32,512]{2,1,0:T(8,128)S(1)}, f32[4,32,512]{2,1,0:T(8,128)S(1)}) fusion(f32[32,512]{1,0:T(8,128)S(1)} %broadcast_add_fusion, f32[4]{0:T(128)S(1)} %fusion.16, f32[32,512]{1,0:T(8,128)S(1)} %get-tuple-element.12, f32[4]{0:T(128)S(1)} %get-tuple-element.18, f32[32,512]{1,0:T(8,128)S(1)} %get-tuple-element.11, f32[4]{0:T(128)S(1)} %get-tuple-element.17), kind=kLoop, calls=%fused_computation.5 | loop fusion | flops 393216 | bytes 720944 | tf_op jit(solution)/shard_map/sin | solution.py:44
  45.7 2.0 %shift.1.refs_4_ = f32[4,2,32,512]{3,2,1,0:T(8,128)} custom-call(s32[16]{0:T(128)S(1)} %copy-done.14, s32[16]{0:T(128)S(1)} %copy-done.15, f32[4,32,512]{2,1,0:T(8,128)S(1)} %get-tuple-element.10.cosine_ref, f32[4,32,512]{2,1,0:T(8,128)S(1)} %get-tuple-element.9.sine_ref, f32[16,2,32,512]{3,2,1,0:T(8,128)S(1)} %fusion.2.interp_ref), custom_call_target="tpu_custom_call" | custom-call | tf_op jit(solution)/shard_map/shift/pallas_call | solution.py:295
  47.7 3.7 %collective-permute-start.1 = (f32[4,2,32,512]{3,2,1,0:T(8,128)}, f32[4,2,32,512]{3,2,1,0:T(8,128)S(1)}, u32[]{:S(2)}, u32[]{:S(2)}) collective-permute-start(f32[4,2,32,512]{3,2,1,0:T(8,128)} %shift.1.refs_4_), channel_id=1, source_target_pairs={{8,0},{16,8},{24,16},{9,1},{17,9},{25,17},{10,2},{18,10},{26,18},{... | collective-permute-start | bytes 1572872 | tf_op jit(solution)/shard_map/ppermute | solution.py:19
  51.4 2.8 %collective-permute-start = (f32[4,2,32,512]{3,2,1,0:T(8,128)}, f32[4,2,32,512]{3,2,1,0:T(8,128)S(1)}, u32[]{:S(2)}, u32[]{:S(2)}) collective-permute-start(f32[4,2,32,512]{3,2,1,0:T(8,128)} %shift.1.refs_4_), channel_id=1, source_target_pairs={{0,8},{8,16},{16,24},{1,9},{9,17},{17,25},{2,10},{10,18},{18,26},{... | collective-permute-start | bytes 1572872 | tf_op jit(solution)/shard_map/ppermute | solution.py:19
  54.2 1.8 %child_translate.1 = f32[16,2,16,256]{3,2,1,0:T(8,128)S(1)} custom-call(s32[16,16]{1,0:T(8,128)S(1)} %copy-done.10, s32[16,16]{1,0:T(8,128)S(1)} %copy-done.11, s32[16]{0:T(128)S(1)} %copy-done.16, f32[16,2,16,256]{3,2,1,0:T(8,128)S(1)} %bitcast.19, f32[16,2,16,256]{3,2,1,0:T(8,128)S(1)} %copy-done.3, f32[16,2,16,256]{3,2,1,0:T(8,128)S(1)} %bitcast.20, ...), custom_call_target="tpu_custom_call" | custom-call | tf_op jit(solution)/shard_map/child_translate/pallas_call | solution.py:241
  56.1 3.3 %collective-permute-done.1.refs_5_ = f32[4,2,32,512]{3,2,1,0:T(8,128)S(1)} collective-permute-done((f32[4,2,32,512]{3,2,1,0:T(8,128)}, f32[4,2,32,512]{3,2,1,0:T(8,128)S(1)}, u32[]{:S(2)}, u32[]{:S(2)}) %collective-permute-start.1) | collective-permute-done | bytes 524320 | tf_op jit(solution)/shard_map/ppermute | solution.py:19
  59.3 1.3 %collective-permute-done.refs_3_ = f32[4,2,32,512]{3,2,1,0:T(8,128)S(1)} collective-permute-done((f32[4,2,32,512]{3,2,1,0:T(8,128)}, f32[4,2,32,512]{3,2,1,0:T(8,128)S(1)}, u32[]{:S(2)}, u32[]{:S(2)}) %collective-permute-start) | collective-permute-done | bytes 524320 | tf_op jit(solution)/shard_map/ppermute | solution.py:19
  60.6 2.4 %parent_translate.1.field_ref = f32[4,2,32,512]{3,2,1,0:T(8,128)} custom-call(s32[4,8]{1,0:T(4,128)S(1)} %copy-done.12, s32[4,8]{1,0:T(4,128)S(1)} %copy-done.13, s32[4]{0:T(128)S(1)} %copy-done.17, f32[4,2,32,512]{3,2,1,0:T(8,128)S(1)} %collective-permute-done.refs_3_, f32[4,2,32,512]{3,2,1,0:T(8,128)S(1)} %copy-done.4, ...), custom_call_target="tpu_custom_call" | custom-call | tf_op jit(solution)/shard_map/parent_translate/pallas_call | solution.py:241
  63.0 0.0 copy-start.5
  63.1 1.0 %copy-done.5 = f32[4,2,32,512]{3,2,1,0:T(8,128)S(1)} copy-done((f32[4,2,32,512]{3,2,1,0:T(8,128)S(1)}, f32[4,2,32,512]{3,2,1,0:T(8,128)}, u32[]{:S(2)}) %copy-start.5) | copy-done | bytes 524312
  64.1 1.1 %unshift.1 = f32[16,2,32,512]{3,2,1,0:T(8,128)S(1)} custom-call(s32[16]{0:T(128)S(1)} %copy-done.14, s32[16]{0:T(128)S(1)} %copy-done.15, f32[4,32,512]{2,1,0:T(8,128)S(1)} %get-tuple-element.10.cosine_ref, f32[4,32,512]{2,1,0:T(8,128)S(1)} %get-tuple-element.9.sine_ref, f32[4,2,32,512]{3,2,1,0:T(8,128)S(1)} %copy-done.5), custom_call_target="tpu_custom_call" | custom-call | tf_op jit(solution)/shard_map/unshift/pallas_call | solution.py:295
  65.2 1.0 %fusion = f32[16,2,32,256]{3,2,1,0:T(8,128)S(1)} fusion(f32[16,2,32,512]{3,2,1,0:T(8,128)S(1)} %unshift.1, f32[256,512]{1,0:T(8,128)S(1)} %copy-done), kind=kOutput, calls=%fused_computation | convolution fusion | flops 805306368 | bytes 3670016 | tf_op jit(solution)/shard_map/ncjg,fg->ncjf/dot_general | solution.py:360
  66.2 34.6 %exchange_1.1 = f32[32,16,256]{2,1,0:T(8,128)S(1)} custom-call(f32[256,128]{1,0:T(8,128)S(1)} %copy-done.9, f32[8,4,32,256]{3,2,1,0:T(8,128)S(1)} %bitcast.15), custom_call_target="tpu_custom_call" | custom-call | tf_op jit(solution)/shard_map/exchange_1/pallas_call | solution.py:173
  100.8 0.9 add.100
  (33 shorter events, 0.2 us)
Async XLA Ops:
  0.6 42.9 %copy-start = (f32[256,512]{1,0:T(8,128)S(1)}, f32[256,512]{1,0:T(8,128)}, u32[]{:S(2)}) copy-start(f32[256,512]{1,0:T(8,128)} %param.17) | copy-start | bytes 1572868
  0.9 1.0 %copy-start.2 = (f32[16,2,16,256]{3,2,1,0:T(8,128)S(1)}, f32[16,2,16,256]{3,2,1,0:T(8,128)}, u32[]{:S(2)}) copy-start(f32[16,2,16,256]{3,2,1,0:T(8,128)} %refs_4_.1) | copy-start | bytes 1572868
  1.9 0.9 copy-start.8
  43.5 2.2 %copy-start.14 = (s32[16]{0:T(128)S(1)}, s32[16]{0:T(128)}, u32[]{:S(2)}) copy-start(s32[16]{0:T(128)} %parent_ref.3) | copy-start | bytes 196
  43.5 2.2 %copy-start.15 = (s32[16]{0:T(128)S(1)}, s32[16]{0:T(128)}, u32[]{:S(2)}) copy-start(s32[16]{0:T(128)} %octant_ref.3) | copy-start | bytes 196
  43.5 10.7 %copy-start.6 = (f32[40,2,16,256]{3,2,1,0:T(8,128)S(1)}, f32[40,2,16,256]{3,2,1,0:T(8,128)}, u32[]{:S(2)}) copy-start(f32[40,2,16,256]{3,2,1,0:T(8,128)} %refs_6_.2) | copy-start | bytes 3932164
  44.5 9.7 %copy-start.3 = (f32[16,2,16,256]{3,2,1,0:T(8,128)S(1)}, f32[16,2,16,256]{3,2,1,0:T(8,128)}, u32[]{:S(2)}) copy-start(f32[16,2,16,256]{3,2,1,0:T(8,128)} %refs_4_.1) | copy-start | bytes 1572868
  44.5 9.7 %copy-start.10 = (s32[16,16]{1,0:T(8,128)S(1)}, s32[16,16]{1,0:T(8,128)}, u32[]{:S(2)}) copy-start(s32[16,16]{1,0:T(8,128)} %refs_0_.2) | copy-start | bytes 3076
  44.6 9.7 %copy-start.11 = (s32[16,16]{1,0:T(8,128)S(1)}, s32[16,16]{1,0:T(8,128)}, u32[]{:S(2)}) copy-start(s32[16,16]{1,0:T(8,128)} %refs_1_.2) | copy-start | bytes 3076
  44.6 9.7 %copy-start.16 = (s32[16]{0:T(128)S(1)}, s32[16]{0:T(128)}, u32[]{:S(2)}) copy-start(s32[16]{0:T(128)} %refs_2_.2) | copy-start | bytes 196
  45.7 14.9 %copy-start.1 = (f32[40,2,32,512]{3,2,1,0:T(8,128)S(1)}, f32[40,2,32,512]{3,2,1,0:T(8,128)}, u32[]{:S(2)}) copy-start(f32[40,2,32,512]{3,2,1,0:T(8,128)} %refs_6_.3) | copy-start | bytes 15728644
  47.7 12.9 %copy-start.4 = (f32[4,2,32,512]{3,2,1,0:T(8,128)S(1)}, f32[4,2,32,512]{3,2,1,0:T(8,128)}, u32[]{:S(2)}) copy-start(f32[4,2,32,512]{3,2,1,0:T(8,128)} %shift.1.refs_4_) | copy-start | bytes 1572868
  47.7 12.9 %copy-start.7 = (f32[4,2,32,512]{3,2,1,0:T(8,128)S(1)}, f32[4,2,32,512]{3,2,1,0:T(8,128)}, u32[]{:S(2)}) copy-start(f32[4,2,32,512]{3,2,1,0:T(8,128)} %refs_7_.1) | copy-start | bytes 1572868
  47.7 12.9 %copy-start.12 = (s32[4,8]{1,0:T(4,128)S(1)}, s32[4,8]{1,0:T(4,128)}, u32[]{:S(2)}) copy-start(s32[4,8]{1,0:T(4,128)} %refs_0_.3) | copy-start | bytes 388
  47.7 12.9 %copy-start.13 = (s32[4,8]{1,0:T(4,128)S(1)}, s32[4,8]{1,0:T(4,128)}, u32[]{:S(2)}) copy-start(s32[4,8]{1,0:T(4,128)} %refs_1_.3) | copy-start | bytes 388
  47.7 12.9 %copy-start.17 = (s32[4]{0:T(128)S(1)}, s32[4]{0:T(128)}, u32[]{:S(2)}) copy-start(s32[4]{0:T(128)} %refs_2_.3) | copy-start | bytes 52
  47.7 11.6 %collective-permute-start.1 = (f32[4,2,32,512]{3,2,1,0:T(8,128)}, f32[4,2,32,512]{3,2,1,0:T(8,128)S(1)}, u32[]{:S(2)}, u32[]{:S(2)}) collective-permute-start(f32[4,2,32,512]{3,2,1,0:T(8,128)} %shift.1.refs_4_), channel_id=1, source_target_pairs={{8,0},{16,8},{24,16},{9,1},{17,9},{25,17},{10,2},{18,10},{26,18},{... | collective-permute-start | bytes 1572872 | tf_op jit(solution)/shard_map/ppermute | solution.py:19
  51.4 9.2 %collective-permute-start = (f32[4,2,32,512]{3,2,1,0:T(8,128)}, f32[4,2,32,512]{3,2,1,0:T(8,128)S(1)}, u32[]{:S(2)}, u32[]{:S(2)}) collective-permute-start(f32[4,2,32,512]{3,2,1,0:T(8,128)} %shift.1.refs_4_), channel_id=1, source_target_pairs={{0,8},{8,16},{16,24},{1,9},{9,17},{17,25},{2,10},{10,18},{18,26},{... | collective-permute-start | bytes 1572872 | tf_op jit(solution)/shard_map/ppermute | solution.py:19
  63.0 1.0 %copy-start.5 = (f32[4,2,32,512]{3,2,1,0:T(8,128)S(1)}, f32[4,2,32,512]{3,2,1,0:T(8,128)}, u32[]{:S(2)}) copy-start(f32[4,2,32,512]{3,2,1,0:T(8,128)} %parent_translate.1.field_ref) | copy-start | bytes 1572868
  65.2 1.0 %copy-start.9 = (f32[256,128]{1,0:T(8,128)S(1)}, f32[256,128]{1,0:T(8,128)}, u32[]{:S(2)}) copy-start(f32[256,128]{1,0:T(8,128)} %matrix_ref.3) | copy-start | bytes 393220
